TPU v7x, 32 devices: a whole 2x2x4 slice. The times are simulated.
32 devices in a mesh: dp: 16 (over z, x, core), tensor: 2 (over y).
Axes of the slice: x: 2, y: 2, z: 4, core: 2. Of those that a mesh axis runs over, the one named last changes fastest.
Arguments:
- tokens: bfloat16 [8192, 1024], P('dp'), may hold values from -6 to 6
- segment_ids: int32 [16, 512], P('dp'), may hold values from 0 to 2, as said below
- mixer_gain: float32 [1024], replicated, may hold values from 0.25 to 1.75
- query_weight: bfloat16 [1024, 1024], P(None, 'tensor'), may hold values from -0.1875 to 0.1875
- key_weight: bfloat16 [1024, 1024], P(None, 'tensor'), may hold values from -0.1875 to 0.1875
- value_weight: bfloat16 [1024, 2048], P(None, 'tensor'), may hold values from -0.1875 to 0.1875
- gate_weight: bfloat16 [1024, 2048], P(None, 'tensor'), may hold values from -0.1875 to 0.1875
- beta_weight: bfloat16 [1024, 8], P(None, 'tensor'), may hold values from -0.1875 to 0.1875
- decay_weight: bfloat16 [1024, 8], P(None, 'tensor'), may hold values from -0.1875 to 0.1875
- query_conv: float32 [4, 1024], P(None, 'tensor'), may hold values from -3 to 3
- key_conv: float32 [4, 1024], P(None, 'tensor'), may hold values from -3 to 3
- value_conv: float32 [4, 2048], P(None, 'tensor'), may hold values from -3 to 3
- decay_log: float32 [8], P('tensor'), may hold values from -7 to -3
- decay_bias: float32 [8], P('tensor'), may hold values from -1.5 to 1.5
- output_gain: float32 [256], replicated, may hold values from 0.25 to 1.75
- out_weight: bfloat16 [2048, 1024], P('tensor'), may hold values from -0.25 to 0.25
- feed_gain: float32 [1024], replicated, may hold values from 0.25 to 1.75
- feed_gate: bfloat16 [1024, 2816], P(None, 'tensor'), may hold values from -0.1875 to 0.1875
- feed_up: bfloat16 [1024, 2816], P(None, 'tensor'), may hold values from -0.1875 to 0.1875
- feed_down: bfloat16 [2816, 1024], P('tensor'), may hold values from -0.21875 to 0.21875
- cotangent: bfloat16 [8192, 1024], P(('dp', 'tensor')), may hold values from -6 to 6
Outputs:
- block_out: bfloat16 [8192, 1024], P(('dp', 'tensor'))
- tokens_grad: bfloat16 [8192, 1024], P(('dp', 'tensor'))
- mixer_gain_grad: float32 [1024], replicated
- query_weight_grad: float32 [1024, 1024], P('dp', 'tensor')
- key_weight_grad: float32 [1024, 1024], P('dp', 'tensor')
- value_weight_grad: float32 [1024, 2048], P('dp', 'tensor')
- gate_weight_grad: float32 [1024, 2048], P('dp', 'tensor')
- beta_weight_grad: float32 [1024, 8], P('dp', 'tensor')
- decay_weight_grad: float32 [1024, 8], P('dp', 'tensor')
- query_conv_grad: float32 [4, 1024], P(None, 'tensor')
- key_conv_grad: float32 [4, 1024], P(None, 'tensor')
- value_conv_grad: float32 [4, 2048], P(None, 'tensor')
- decay_log_grad: float32 [8], P('tensor')
- decay_bias_grad: float32 [8], P('tensor')
- output_gain_grad: float32 [256], replicated
- out_weight_grad: float32 [2048, 1024], P('tensor', 'dp')
- feed_gain_grad: float32 [1024], replicated
- feed_gate_grad: float32 [1024, 2816], P('dp', 'tensor')
- feed_up_grad: float32 [1024, 2816], P('dp', 'tensor')
- feed_down_grad: float32 [2816, 1024], P('tensor', 'dp')
Inputs may be any that keep to these rules, and one draw needn't show every extreme that they name: `segment_ids`: in each of the 16 rows the id is 0 at the first token, never falls, and rises by one at each document start; every row holds two or three documents.
All inputs are finite; a program needn't handle non-finite values.
Results may differ from a plain program's by a relative error of at most 0.017.
Values may be sent and summed in bfloat16 or wider, within the bound.
A program may use at most 256 MiB of HBM per device.

v0:
```python
import jax
import jax.numpy as jnp
from jax import lax
from jax.sharding import PartitionSpec as P

BLOCK = 64


EPSILON = 1e-06
PRECISE = lax.Precision.HIGHEST


def norm_forward(values, gain_row):
    factor = lax.rsqrt(jnp.mean(values * values, axis=-1, keepdims=True) + EPSILON)
    return (values * factor * gain_row, factor)


def norm_backward(upstream, values, factor, gain_row):
    unit_scaled = values * factor
    weighted = upstream * gain_row
    backward = factor * (
        weighted - unit_scaled * jnp.mean(weighted * unit_scaled, axis=-1, keepdims=True)
    )
    return (backward, upstream * unit_scaled)


def silu_slope(argument):
    logistic = jax.nn.sigmoid(argument)
    return logistic * (1.0 + argument * (1.0 - logistic))


def dot_first(left, right):
    return lax.dot_general(
        left, right, (((0,), (0,)), ((), ())), preferred_element_type=jnp.float32
    )


def dot_last(left, right):
    return lax.dot_general(
        left, right, (((1,), (1,)), ((), ())), preferred_element_type=jnp.float32
    )


def take_rows(source, first_row, row_share):
    return lax.dynamic_slice_in_dim(source, first_row, row_share, 0)


def same_mask(segments, taps):
    length = segments.shape[1]
    columns = []
    for offset in range(taps):
        shifted = jnp.pad(segments, ((0, 0), (offset, 0)), constant_values=-1)[:, :length]
        columns.append((shifted == segments).astype(jnp.float32))
    return jnp.stack(columns, axis=-1)


def short_conv(values, weight, live_mask):
    length = values.shape[1]
    summed = values * weight[0] * live_mask[..., 0:1]
    for offset in range(1, weight.shape[0]):
        shifted = jnp.pad(values, ((0, 0), (offset, 0), (0, 0)))[:, :length]
        summed = summed + shifted * weight[offset] * live_mask[..., offset : offset + 1]
    return summed


def delta_rule(queries, key_vecs, values, beta_rate, log_decay, segments, block_size):
    seq_count, length, head_count, key_dim = queries.shape
    value_dim = values.shape[-1]
    block_count = length // block_size

    def blocks(source):
        shaped = source.reshape((seq_count, block_count, block_size) + source.shape[2:])
        return jnp.moveaxis(shaped, 1, 0)

    segment_blocks = blocks(segments)
    previous = jnp.concatenate(
        [jnp.full((1, seq_count), -1, jnp.int32), segment_blocks[:-1, :, block_size - 1]], axis=0
    )
    row_index = lax.broadcasted_iota(jnp.int32, (block_size, block_size), 0)
    col_index = lax.broadcasted_iota(jnp.int32, (block_size, block_size), 1)
    inclusive = row_index >= col_index
    strictly = row_index > col_index

    def advance(memory, inputs):
        query_block, key_block, value_block, beta_block, decay_block, seg_block, prev_block = inputs
        query_heads = jnp.moveaxis(query_block, 2, 1)
        key_heads = jnp.moveaxis(key_block, 2, 1)
        value_heads = jnp.moveaxis(value_block, 2, 1)
        beta_heads = jnp.moveaxis(beta_block, 2, 1)
        cumulative = jnp.cumsum(jnp.moveaxis(decay_block, 2, 1), axis=-1)
        same_doc = (seg_block[:, :, None] == seg_block[:, None, :])[:, None]
        keep_mask = jnp.logical_and(inclusive, same_doc)
        spread = cumulative[..., :, None] - cumulative[..., None, :]
        within = jnp.where(keep_mask, jnp.exp(jnp.where(keep_mask, spread, 0.0)), 0.0)
        fresh_mask = (seg_block == prev_block[:, None])[:, None, :]
        start_decay = jnp.where(fresh_mask, jnp.exp(cumulative), 0.0)
        last_seg = seg_block[:, block_size - 1]
        tail_mask = (seg_block == last_seg[:, None])[:, None, :]
        end_decay = jnp.where(
            tail_mask, jnp.exp(cumulative[..., block_size - 1 :] - cumulative), 0.0
        )
        carried = jnp.where(
            (last_seg == prev_block)[:, None], jnp.exp(cumulative[..., block_size - 1]), 0.0
        )
        key_gram = jnp.einsum("bhid,bhjd->bhij", key_heads, key_heads, precision=PRECISE)
        lower_part = jnp.where(strictly, key_gram * within, 0.0) * beta_heads[..., None]
        recalled = jnp.einsum("bhid,bhde->bhie", key_heads, memory, precision=PRECISE)
        target = beta_heads[..., None] * (value_heads - start_decay[..., None] * recalled)
        update = jax.scipy.linalg.solve_triangular(
            lower_part, target, lower=True, unit_diagonal=True
        )
        scores = jnp.einsum("bhid,bhjd->bhij", query_heads, key_heads, precision=PRECISE) * within
        output = start_decay[..., None] * jnp.einsum(
            "bhid,bhde->bhie", query_heads, memory, precision=PRECISE
        )
        output = output + jnp.einsum("bhij,bhje->bhie", scores, update, precision=PRECISE)
        memory = carried[..., None, None] * memory + jnp.einsum(
            "bhjd,bhje->bhde", key_heads * end_decay[..., None], update, precision=PRECISE
        )
        return (memory, output)

    initial = jnp.zeros((seq_count, head_count, key_dim, value_dim), jnp.float32)
    final_memory, outputs = lax.scan(
        advance,
        initial,
        (
            blocks(queries),
            blocks(key_vecs),
            blocks(values),
            blocks(beta_rate),
            blocks(log_decay),
            segment_blocks,
            previous,
        ),
    )
    return jnp.transpose(outputs, (1, 0, 3, 2, 4)).reshape(seq_count, length, head_count, value_dim)


def mixer_local(
    query_pre,
    key_pre,
    value_pre,
    gate_pre,
    beta_pre,
    decay_pre,
    query_conv,
    key_conv,
    value_conv,
    decay_log,
    decay_bias,
    output_gain,
    segments,
    key_dim,
    block_size,
):
    seq_count, length = segments.shape
    head_count = decay_log.shape[0]
    value_dim = output_gain.shape[0]
    live_mask = same_mask(segments, query_conv.shape[0])
    queries = jax.nn.silu(short_conv(query_pre, query_conv, live_mask)).reshape(
        seq_count, length, head_count, key_dim
    )
    queries = (
        queries
        * lax.rsqrt(jnp.sum(queries * queries, axis=-1, keepdims=True) + EPSILON)
        * key_dim ** (-0.5)
    )
    key_vecs = jax.nn.silu(short_conv(key_pre, key_conv, live_mask)).reshape(
        seq_count, length, head_count, key_dim
    )
    key_vecs = key_vecs * lax.rsqrt(jnp.sum(key_vecs * key_vecs, axis=-1, keepdims=True) + EPSILON)
    values = jax.nn.silu(short_conv(value_pre, value_conv, live_mask)).reshape(
        seq_count, length, head_count, value_dim
    )
    beta_rate = jax.nn.sigmoid(beta_pre)
    log_decay = -jnp.exp(decay_log) * jax.nn.softplus(decay_pre + decay_bias)
    recurrent = delta_rule(queries, key_vecs, values, beta_rate, log_decay, segments, block_size)
    normed = recurrent * lax.rsqrt(
        jnp.mean(recurrent * recurrent, axis=-1, keepdims=True) + EPSILON
    )
    gated_out = (
        normed
        * output_gain
        * jax.nn.silu(gate_pre.reshape(seq_count, length, head_count, value_dim))
    )
    return gated_out.reshape(seq_count, length, head_count * value_dim)


def per_device(
    tokens,
    segment_ids,
    mixer_gain,
    query_weight,
    key_weight,
    value_weight,
    gate_weight,
    beta_weight,
    decay_weight,
    query_conv,
    key_conv,
    value_conv,
    decay_log,
    decay_bias,
    output_gain,
    out_weight,
    feed_gain,
    feed_gate,
    feed_up,
    feed_down,
    cotangent,
):
    seq_count, length = segment_ids.shape
    total_rows = seq_count * length
    row_share = total_rows // lax.axis_size("tensor")
    first_row = lax.axis_index("tensor") * row_share
    projections = (query_weight, key_weight, value_weight, gate_weight, beta_weight, decay_weight)
    key_dim = query_weight.shape[1] // decay_log.shape[0]
    inputs_float = tokens.astype(jnp.float32)
    normed_first, factor_first = norm_forward(inputs_float, mixer_gain)
    normed_in = normed_first.astype(jnp.bfloat16)
    projected = [
        jnp.dot(normed_in, weight, preferred_element_type=jnp.float32).reshape(
            seq_count, length, -1
        )
        for weight in projections
    ]

    def mixer_apply(*members):
        return mixer_local(*members, segment_ids, key_dim, BLOCK)

    gated_out, mixer_back = jax.vjp(
        mixer_apply,
        *projected,
        query_conv,
        key_conv,
        value_conv,
        decay_log,
        decay_bias,
        output_gain
    )
    gated_low = gated_out.reshape(total_rows, -1).astype(jnp.bfloat16)
    mixer_part = jnp.dot(gated_low, out_weight, preferred_element_type=jnp.float32)
    mixed_all = lax.psum(mixer_part, "tensor")
    middle = inputs_float + mixed_all
    normed_second, factor_second = norm_forward(middle, feed_gain)
    normed_mid = normed_second.astype(jnp.bfloat16)
    middle_rows = take_rows(middle, first_row, row_share)
    swish_in = jnp.dot(normed_mid, feed_gate, preferred_element_type=jnp.float32)
    linear_up = jnp.dot(normed_mid, feed_up, preferred_element_type=jnp.float32)
    hidden = (jax.nn.silu(swish_in) * linear_up).astype(jnp.bfloat16)
    feed_part = jnp.dot(hidden, feed_down, preferred_element_type=jnp.float32)
    feed_rows = lax.psum_scatter(
        feed_part.astype(jnp.bfloat16), "tensor", scatter_dimension=0, tiled=True
    ).astype(jnp.float32)
    block_out = (middle_rows + feed_rows).astype(jnp.bfloat16)
    cotangent_all = lax.all_gather(cotangent, "tensor", axis=0, tiled=True)
    downward_grad = dot_first(hidden, cotangent_all)
    grad_hidden = dot_last(cotangent_all, feed_down)
    swish_grad = (grad_hidden * linear_up * silu_slope(swish_in)).astype(jnp.bfloat16)
    linear_grad = (grad_hidden * jax.nn.silu(swish_in)).astype(jnp.bfloat16)
    gating_grad = dot_first(normed_mid, swish_grad)
    upward_grad = dot_first(normed_mid, linear_grad)
    second_part = dot_last(swish_grad, feed_gate) + dot_last(linear_grad, feed_up)
    grad_second = lax.psum(second_part, "tensor")
    back_second, second_terms = norm_backward(grad_second, middle, factor_second, feed_gain)
    gain_second = jnp.sum(take_rows(second_terms, first_row, row_share), axis=0)
    grad_middle_full = cotangent_all.astype(jnp.float32) + back_second
    grad_middle_rows = take_rows(grad_middle_full, first_row, row_share)
    grad_middle_low = grad_middle_full.astype(jnp.bfloat16)
    outward_grad = dot_first(gated_low, grad_middle_low)
    grad_gated = dot_last(grad_middle_low, out_weight)
    mixer_grads = mixer_back(grad_gated.reshape(seq_count, length, -1))
    low_grads = [member.reshape(total_rows, -1).astype(jnp.bfloat16) for member in mixer_grads[:6]]
    proj_grads = [dot_first(normed_in, member) for member in low_grads]
    first_part = dot_last(low_grads[0], projections[0])
    for index_proj in range(1, 6):
        first_part = first_part + dot_last(low_grads[index_proj], projections[index_proj])
    grad_first = lax.psum_scatter(first_part, "tensor", scatter_dimension=0, tiled=True)
    back_first, first_terms = norm_backward(
        grad_first,
        take_rows(inputs_float, first_row, row_share),
        take_rows(factor_first, first_row, row_share),
        mixer_gain,
    )
    gain_first = jnp.sum(first_terms, axis=0)
    tokens_grad = (grad_middle_rows + back_first).astype(jnp.bfloat16)
    gain_sums = lax.psum((gain_first, gain_second, mixer_grads[11]), ("dp", "tensor"))
    head_sums = lax.psum(
        (mixer_grads[6], mixer_grads[7], mixer_grads[8], mixer_grads[9], mixer_grads[10]), "dp"
    )
    every_sum = (
        lax.psum_scatter(
            proj_grads[0].astype(jnp.bfloat16), "dp", scatter_dimension=0, tiled=True
        ).astype(jnp.float32),
        lax.psum_scatter(
            proj_grads[1].astype(jnp.bfloat16), "dp", scatter_dimension=0, tiled=True
        ).astype(jnp.float32),
        lax.psum_scatter(
            proj_grads[2].astype(jnp.bfloat16), "dp", scatter_dimension=0, tiled=True
        ).astype(jnp.float32),
        lax.psum_scatter(
            proj_grads[3].astype(jnp.bfloat16), "dp", scatter_dimension=0, tiled=True
        ).astype(jnp.float32),
        lax.psum_scatter(
            proj_grads[4].astype(jnp.bfloat16), "dp", scatter_dimension=0, tiled=True
        ).astype(jnp.float32),
        lax.psum_scatter(
            proj_grads[5].astype(jnp.bfloat16), "dp", scatter_dimension=0, tiled=True
        ).astype(jnp.float32),
        lax.psum_scatter(
            outward_grad.astype(jnp.bfloat16), "dp", scatter_dimension=1, tiled=True
        ).astype(jnp.float32),
        lax.psum_scatter(
            gating_grad.astype(jnp.bfloat16), "dp", scatter_dimension=0, tiled=True
        ).astype(jnp.float32),
        lax.psum_scatter(
            upward_grad.astype(jnp.bfloat16), "dp", scatter_dimension=0, tiled=True
        ).astype(jnp.float32),
        lax.psum_scatter(
            downward_grad.astype(jnp.bfloat16), "dp", scatter_dimension=1, tiled=True
        ).astype(jnp.float32),
    )
    mixer_sums = every_sum[:7]
    feed_sums = every_sum[7:]
    return (
        block_out,
        tokens_grad,
        gain_sums[0],
        mixer_sums[0],
        mixer_sums[1],
        mixer_sums[2],
        mixer_sums[3],
        mixer_sums[4],
        mixer_sums[5],
        head_sums[0],
        head_sums[1],
        head_sums[2],
        head_sums[3],
        head_sums[4],
        gain_sums[2],
        mixer_sums[6],
        gain_sums[1],
        feed_sums[0],
        feed_sums[1],
        feed_sums[2],
    )


def solution(mesh):
    in_specs = (
        P("dp", None),
        P("dp", None),
        P(),
        P(None, "tensor"),
        P(None, "tensor"),
        P(None, "tensor"),
        P(None, "tensor"),
        P(None, "tensor"),
        P(None, "tensor"),
        P(None, "tensor"),
        P(None, "tensor"),
        P(None, "tensor"),
        P("tensor"),
        P("tensor"),
        P(),
        P("tensor", None),
        P(),
        P(None, "tensor"),
        P(None, "tensor"),
        P("tensor", None),
        P(("dp", "tensor"), None),
    )
    out_specs = (
        P(("dp", "tensor"), None),
        P(("dp", "tensor"), None),
        P(),
        P("dp", "tensor"),
        P("dp", "tensor"),
        P("dp", "tensor"),
        P("dp", "tensor"),
        P("dp", "tensor"),
        P("dp", "tensor"),
        P(None, "tensor"),
        P(None, "tensor"),
        P(None, "tensor"),
        P("tensor"),
        P("tensor"),
        P(),
        P("tensor", "dp"),
        P(),
        P("dp", "tensor"),
        P("dp", "tensor"),
        P("tensor", "dp"),
    )
    return jax.shard_map(
        per_device, mesh=mesh, in_specs=in_specs, out_specs=out_specs, check_vma=False
    )
```

profile of v0, /device:TPU:0, one launch (start us, length us, event | category | flops | bytes accessed | tf_op | source)
XLA Modules:
  0.0 1856.7 jit_solution(11806578818085093433)
XLA Ops:
  12.5 3.1 fusion.229
  18.0 2.6 reshape.2155
  39.0 3.2 fusion.232
  42.3 3.3 fusion.182
  45.7 3.2 reshape.2158
  61.8 420.3 %while.101 = (s32[]{:T(128)}, f32[1,4,128,256]{3,2,1,0:T(8,128)S(1)}, f32[8,1,4,64,256]{4,3,2,1,0:T(8,128)}, pred[8,1,4,64,64]{4,3,2,1,0:T(32,128)(4,1)}, f32[8,...) while((s32[]{:T(128)}, ...), condition=%wide.region_5.6_spmd.clone, body=%wide.region_3.5_spmd.clone.sunk | while | flops 454780608 | bytes 12164122 | solution.py:123
  77.2 21.0 %custom-call.58 = f32[4,1,64,64]{2,3,1,0:T(8,128)} custom-call(f32[4,1,64,64]{3,2,1,0:T(8,128)} %add_bitcast_fusion.4), custom_call_target="InvertDiagBlocksLowerTriangular" | custom-call | tf_op jit(solution)/shard_map/jvp()/while/body/eval_jaxpr/jit(_solve_triangular)/vmap()/triangular_solve | solution.py:109
  129.6 21.0 %custom-call.58 = f32[4,1,64,64]{2,3,1,0:T(8,128)} custom-call(f32[4,1,64,64]{3,2,1,0:T(8,128)} %add_bitcast_fusion.4), custom_call_target="InvertDiagBlocksLowerTriangular" | custom-call | tf_op jit(solution)/shard_map/jvp()/while/body/eval_jaxpr/jit(_solve_triangular)/vmap()/triangular_solve | solution.py:109
  182.2 21.0 %custom-call.58 = f32[4,1,64,64]{2,3,1,0:T(8,128)} custom-call(f32[4,1,64,64]{3,2,1,0:T(8,128)} %add_bitcast_fusion.4), custom_call_target="InvertDiagBlocksLowerTriangular" | custom-call | tf_op jit(solution)/shard_map/jvp()/while/body/eval_jaxpr/jit(_solve_triangular)/vmap()/triangular_solve | solution.py:109
  234.7 21.0 %custom-call.58 = f32[4,1,64,64]{2,3,1,0:T(8,128)} custom-call(f32[4,1,64,64]{3,2,1,0:T(8,128)} %add_bitcast_fusion.4), custom_call_target="InvertDiagBlocksLowerTriangular" | custom-call | tf_op jit(solution)/shard_map/jvp()/while/body/eval_jaxpr/jit(_solve_triangular)/vmap()/triangular_solve | solution.py:109
  287.2 21.0 %custom-call.58 = f32[4,1,64,64]{2,3,1,0:T(8,128)} custom-call(f32[4,1,64,64]{3,2,1,0:T(8,128)} %add_bitcast_fusion.4), custom_call_target="InvertDiagBlocksLowerTriangular" | custom-call | tf_op jit(solution)/shard_map/jvp()/while/body/eval_jaxpr/jit(_solve_triangular)/vmap()/triangular_solve | solution.py:109
  339.7 21.0 %custom-call.58 = f32[4,1,64,64]{2,3,1,0:T(8,128)} custom-call(f32[4,1,64,64]{3,2,1,0:T(8,128)} %add_bitcast_fusion.4), custom_call_target="InvertDiagBlocksLowerTriangular" | custom-call | tf_op jit(solution)/shard_map/jvp()/while/body/eval_jaxpr/jit(_solve_triangular)/vmap()/triangular_solve | solution.py:109
  392.2 21.0 %custom-call.58 = f32[4,1,64,64]{2,3,1,0:T(8,128)} custom-call(f32[4,1,64,64]{3,2,1,0:T(8,128)} %add_bitcast_fusion.4), custom_call_target="InvertDiagBlocksLowerTriangular" | custom-call | tf_op jit(solution)/shard_map/jvp()/while/body/eval_jaxpr/jit(_solve_triangular)/vmap()/triangular_solve | solution.py:109
  444.7 21.0 %custom-call.58 = f32[4,1,64,64]{2,3,1,0:T(8,128)} custom-call(f32[4,1,64,64]{3,2,1,0:T(8,128)} %add_bitcast_fusion.4), custom_call_target="InvertDiagBlocksLowerTriangular" | custom-call | tf_op jit(solution)/shard_map/jvp()/while/body/eval_jaxpr/jit(_solve_triangular)/vmap()/triangular_solve | solution.py:109
  490.8 3.0 multiply_convert_fusion.4
  494.8 2.6 fusion.246
  498.4 64.8 %all-reduce.40.cloned.1.call-done = f32[512,1024]{1,0:T(8,128)} async-done(((f32[512,1024]{1,0:T(8,128)}), f32[512,1024]{1,0:T(8,128)}) %all-reduce.40.cloned.1.call-update) | async-done | bytes 2097168 | tf_op jit(solution)/shard_map/psum | solution.py:243
  569.2 3.4 fusion.247
  572.6 3.4 fusion.248
  576.0 10.1 all-gather.2.cloned.1.call-done
  586.1 6.9 multiply_convert_fusion
  595.9 3.3 convolution_add_fusion.3
  600.7 3.2 reshape_reshape.7
  603.9 2.6 mul.1648
  606.5 2.7 mul.1649
  609.3 4.2 convolution_convert_fusion.6
  613.5 48.8 %all-reduce.42.cloned.1.call-done = f32[512,1024]{1,0:T(8,128)} async-done(((f32[512,1024]{1,0:T(8,128)}), f32[512,1024]{1,0:T(8,128)}) %all-reduce.42.cloned.1.call-update) | async-done | bytes 2097168 | tf_op jit(solution)/shard_map/psum | solution.py:264
  662.3 2.7 multiply_reduce_fusion.7
  669.0 5.9 fusion.179
  674.9 3.9 reshape_reshape.6
  678.8 3.6 multiply_reduce_fusion.1
  687.2 423.4 %while.102 = (s32[]{:T(128)}, f32[1,4,128,256]{2,3,1,0:T(8,128)S(1)}, f32[8,1,64,4,128]{4,2,3,1,0:T(8,128)S(1)}, f32[8,1,64,4,128]{4,2,3,1,0:T(8,128)}, f32[8,1,...) while((s32[]{:T(128)}, ...), condition=%wide.region_24.25_spmd.clone, body=%wide.region_13.24_spmd.clone.sunk | while | flops 921532480 | bytes 18302968 | solution.py:123
  692.5 19.7 %custom-call.59 = f32[4,1,64,64]{2,3,1,0:T(8,128)S(1)} custom-call(f32[4,1,64,64]{3,2,1,0:T(8,128)S(1)} %add_bitcast_fusion.5), custom_call_target="InvertDiagBlocksLowerTriangular" | custom-call | tf_op jit(solution)/shard_map/transpose(jvp())/while/body/eval_jaxpr/jit(_solve_triangular)/vmap()/triangular_solve | solution.py:109
  745.4 19.7 %custom-call.59 = f32[4,1,64,64]{2,3,1,0:T(8,128)S(1)} custom-call(f32[4,1,64,64]{3,2,1,0:T(8,128)S(1)} %add_bitcast_fusion.5), custom_call_target="InvertDiagBlocksLowerTriangular" | custom-call | tf_op jit(solution)/shard_map/transpose(jvp())/while/body/eval_jaxpr/jit(_solve_triangular)/vmap()/triangular_solve | solution.py:109
  798.3 19.7 %custom-call.59 = f32[4,1,64,64]{2,3,1,0:T(8,128)S(1)} custom-call(f32[4,1,64,64]{3,2,1,0:T(8,128)S(1)} %add_bitcast_fusion.5), custom_call_target="InvertDiagBlocksLowerTriangular" | custom-call | tf_op jit(solution)/shard_map/transpose(jvp())/while/body/eval_jaxpr/jit(_solve_triangular)/vmap()/triangular_solve | solution.py:109
  851.2 19.7 %custom-call.59 = f32[4,1,64,64]{2,3,1,0:T(8,128)S(1)} custom-call(f32[4,1,64,64]{3,2,1,0:T(8,128)S(1)} %add_bitcast_fusion.5), custom_call_target="InvertDiagBlocksLowerTriangular" | custom-call | tf_op jit(solution)/shard_map/transpose(jvp())/while/body/eval_jaxpr/jit(_solve_triangular)/vmap()/triangular_solve | solution.py:109
  904.1 19.7 %custom-call.59 = f32[4,1,64,64]{2,3,1,0:T(8,128)S(1)} custom-call(f32[4,1,64,64]{3,2,1,0:T(8,128)S(1)} %add_bitcast_fusion.5), custom_call_target="InvertDiagBlocksLowerTriangular" | custom-call | tf_op jit(solution)/shard_map/transpose(jvp())/while/body/eval_jaxpr/jit(_solve_triangular)/vmap()/triangular_solve | solution.py:109
  957.0 19.7 %custom-call.59 = f32[4,1,64,64]{2,3,1,0:T(8,128)S(1)} custom-call(f32[4,1,64,64]{3,2,1,0:T(8,128)S(1)} %add_bitcast_fusion.5), custom_call_target="InvertDiagBlocksLowerTriangular" | custom-call | tf_op jit(solution)/shard_map/transpose(jvp())/while/body/eval_jaxpr/jit(_solve_triangular)/vmap()/triangular_solve | solution.py:109
  1009.9 19.7 %custom-call.59 = f32[4,1,64,64]{2,3,1,0:T(8,128)S(1)} custom-call(f32[4,1,64,64]{3,2,1,0:T(8,128)S(1)} %add_bitcast_fusion.5), custom_call_target="InvertDiagBlocksLowerTriangular" | custom-call | tf_op jit(solution)/shard_map/transpose(jvp())/while/body/eval_jaxpr/jit(_solve_triangular)/vmap()/triangular_solve | solution.py:109
  1062.8 19.7 %custom-call.59 = f32[4,1,64,64]{2,3,1,0:T(8,128)S(1)} custom-call(f32[4,1,64,64]{3,2,1,0:T(8,128)S(1)} %add_bitcast_fusion.5), custom_call_target="InvertDiagBlocksLowerTriangular" | custom-call | tf_op jit(solution)/shard_map/transpose(jvp())/while/body/eval_jaxpr/jit(_solve_triangular)/vmap()/triangular_solve | solution.py:109
  1124.4 2.8 transpose.268
  1130.2 4.6 multiply_reduce_fusion.18
  1136.3 3.2 multiply_multiply_fusion.7
  1149.9 4.8 convolution_convert_fusion.1
  1154.8 4.8 convolution_convert_fusion.2
  1160.8 4.8 convolution_convert_fusion
  1167.2 3.9 convolution_convert_fusion.3
  1171.2 3.4 transpose.270
  1174.6 3.7 multiply_reduce_fusion.5
  1180.3 2.7 convolution_convert_fusion.5
  1184.2 2.8 convolution_convert_fusion.4
  1197.6 3.0 convert_element_type.149
  1200.7 61.5 %all-reduce.36 = (f32[4,512]{1,0:T(4,128)}, f32[4,512]{1,0:T(4,128)}, f32[4,1024]{1,0:T(4,128)}, f32[4]{0:T(128)}, f32[4]{0:T(128)}) all-reduce(f32[4,512]{1,0:T(4,128)S(1)} %pad_add_fusion.2, f32[4,512]{1,0:T(4,128)S(1)} %pad_add_fusion.1, f32[4,1024]{1,0:T(4,128)S(1)} %pad_add_fusion, ...), channel_id=1, replica_groups=mesh['dp'=16,'tensor'=2] {'dp'}, use_global_device_ids=true, to_apply=%region_41.42 | all-reduce | flops 8200 | bytes 65600 | tf_op jit(solution)/shard_map/psum | solution.py:288
  1268.7 45.8 %reduce-scatter.23.cloned.1.call-done = bf16[64,512]{1,0:T(8,128)(2,1)} async-done(((bf16[1024,512]{1,0:T(8,128)(2,1)}), bf16[64,512]{1,0:T(8,128)(2,1)}) %reduce-scatter.23.cloned.1.call-update) | async-done | bytes 65552 | tf_op jit(solution)/shard_map/reduce_scatter | solution.py:295
  1316.0 58.8 %reduce-scatter.21.cloned.1.call-done = bf16[64,512]{1,0:T(8,128)(2,1)} async-done(((bf16[1024,512]{1,0:T(8,128)(2,1)}), bf16[64,512]{1,0:T(8,128)(2,1)}) %reduce-scatter.21.cloned.1.call-update) | async-done | bytes 65552 | tf_op jit(solution)/shard_map/reduce_scatter | solution.py:292
  1376.3 66.6 %reduce-scatter.33.cloned.1.call-done = bf16[64,1408]{1,0:T(8,128)(2,1)} async-done(((bf16[1024,1408]{1,0:T(8,128)(2,1)}), bf16[64,1408]{1,0:T(8,128)(2,1)}) %reduce-scatter.33.cloned.1.call-update) | async-done | bytes 180240 | tf_op jit(solution)/shard_map/reduce_scatter | solution.py:316
  1444.6 66.2 %reduce-scatter.31.cloned.1.call-done = bf16[64,1408]{1,0:T(8,128)(2,1)} async-done(((bf16[1024,1408]{1,0:T(8,128)(2,1)}), bf16[64,1408]{1,0:T(8,128)(2,1)}) %reduce-scatter.31.cloned.1.call-update) | async-done | bytes 180240 | tf_op jit(solution)/shard_map/reduce_scatter | solution.py:313
  1512.5 66.4 %reduce-scatter.35.cloned.1.call-done = bf16[1408,64]{0,1:T(8,128)(2,1)} async-done(((bf16[1408,1024]{0,1:T(8,128)(2,1)}), bf16[1408,64]{0,1:T(8,128)(2,1)}) %reduce-scatter.35.cloned.1.call-update) | async-done | bytes 180240 | tf_op jit(solution)/shard_map/reduce_scatter | solution.py:319
  1580.6 62.9 %reduce-scatter.29.cloned.1.call-done = bf16[1024,64]{0,1:T(8,128)(2,1)} async-done(((bf16[1024,1024]{0,1:T(8,128)(2,1)}), bf16[1024,64]{0,1:T(8,128)(2,1)}) %reduce-scatter.29.cloned.1.call-update) | async-done | bytes 131088 | tf_op jit(solution)/shard_map/reduce_scatter | solution.py:310
  1645.1 62.9 %reduce-scatter.25.cloned.1.call-done = bf16[64,1024]{1,0:T(8,128)(2,1)} async-done(((bf16[1024,1024]{1,0:T(8,128)(2,1)}), bf16[64,1024]{1,0:T(8,128)(2,1)}) %reduce-scatter.25.cloned.1.call-update) | async-done | bytes 131088 | tf_op jit(solution)/shard_map/reduce_scatter | solution.py:298
  1709.6 62.7 %reduce-scatter.27.cloned.1.call-done = bf16[64,1024]{1,0:T(8,128)(2,1)} async-done(((bf16[1024,1024]{1,0:T(8,128)(2,1)}), bf16[64,1024]{1,0:T(8,128)(2,1)}) %reduce-scatter.27.cloned.1.call-update) | async-done | bytes 131088 | tf_op jit(solution)/shard_map/reduce_scatter | solution.py:301
  1773.9 31.3 %reduce-scatter.19.cloned.1.call-done = f32[256,1024]{1,0:T(8,128)} async-done(((f32[512,1024]{1,0:T(8,128)}), f32[256,1024]{1,0:T(8,128)}) %reduce-scatter.19.cloned.1.call-update) | async-done | bytes 1048592 | tf_op jit(solution)/shard_map/reduce_scatter | solution.py:278
  1807.3 39.5 %all-reduce.35 = (f32[1024]{0:T(1024)}, f32[256]{0:T(256)}, f32[1024]{0:T(1024)}) all-reduce(f32[1024]{0:T(1024)S(1)} %get-tuple-element.2221, f32[256]{0:T(256)S(1)} %get-tuple-element.2216, f32[1024]{0:T(1024)S(1)} %fusion.200), channel_id=1, replica_groups=mesh['dp'=16,'tensor'=2] {'dp','tensor'}, use_global_device_ids=true, to_apply=%region_30.31 | all-reduce | flops 2304 | bytes 18432 | tf_op jit(solution)/shard_map/psum | solution.py:287
  1846.8 2.9 add_convert_fusion
  (1251 shorter events, 640.2 us)
Async XLA Ops:
  7.2 578.9 %copy-start = (bf16[1408,1024]{1,0:T(8,128)(2,1)S(1)}, bf16[1408,1024]{1,0:T(8,128)(2,1)}, u32[]{:S(2)}) copy-start(bf16[1408,1024]{1,0:T(8,128)(2,1)} %param.44) | copy-start | bytes 8650756
  7.2 556.0 %all-reduce.40.cloned.1.call-start = ((), (), s32[]{:S(2)}) async-start(), calls=%async_computation.12 | async-start | bytes 4194304 | tf_op jit(solution)/shard_map/psum | solution.py:243
  9.0 43.0 %copy-start.107 = (f32[512]{0:T(512)}, f32[512]{0:T(512)S(1)}, u32[]{:S(2)}) copy-start(f32[512]{0:T(512)S(1)} %add_rsqrt_fusion.3) | copy-start | bytes 6148
  12.4 29.9 %copy-start.54 = (f32[1,512]{1,0:T(1,128)}, f32[1,512]{1,0:T(1,128)S(1)}, u32[]{:S(2)}) copy-start(f32[1,512]{1,0:T(1,128)S(1)} %get-tuple-element.2486) | copy-start | bytes 6148
  12.4 29.9 %copy-start.56 = (f32[1,512]{1,0:T(1,128)}, f32[1,512]{1,0:T(1,128)S(1)}, u32[]{:S(2)}) copy-start(f32[1,512]{1,0:T(1,128)S(1)} %get-tuple-element.2487) | copy-start | bytes 6148
  12.4 29.9 %copy-start.58 = (f32[1,512]{1,0:T(1,128)}, f32[1,512]{1,0:T(1,128)S(1)}, u32[]{:S(2)}) copy-start(f32[1,512]{1,0:T(1,128)S(1)} %get-tuple-element.2488) | copy-start | bytes 6148
  35.1 7.1 copy-start.60
  35.1 7.1 copy-start.62
  45.7 6.2 copy-start.99
  49.0 10.9 copy-start.109
  53.6 7.6 copy-start.75
  64.5 8.9 copy-start.48
  105.8 6.9 copy-start.97
  105.8 7.4 copy-start.96
  105.8 8.0 copy-start.122
  117.0 8.9 copy-start.48
  157.2 6.2 copy-start.46
  157.2 6.2 copy-start.49
  157.2 6.2 copy-start.53
  158.3 6.9 copy-start.97
  158.3 7.5 copy-start.96
  158.3 8.0 copy-start.122
  169.6 8.9 copy-start.48
  210.8 6.9 copy-start.97
  210.8 7.4 copy-start.96
  210.8 8.0 copy-start.122
  222.1 8.9 copy-start.48
  263.4 6.9 copy-start.97
  263.4 7.5 copy-start.96
  263.4 8.0 copy-start.122
  274.6 8.9 copy-start.48
  315.9 6.9 copy-start.97
  315.9 7.4 copy-start.96
  315.9 8.0 copy-start.122
  327.1 8.9 copy-start.48
  368.4 6.9 copy-start.97
  368.4 7.5 copy-start.96
  368.4 8.0 copy-start.122
  379.7 8.9 copy-start.48
  420.9 6.9 copy-start.97
  420.9 7.5 copy-start.96
  420.9 7.9 copy-start.122
  432.1 8.9 copy-start.48
  473.4 6.9 copy-start.97
  473.4 7.4 copy-start.96
  473.4 8.0 copy-start.122
  497.4 88.7 %all-gather.2.cloned.1.call-start = ((), (), s32[]{:S(2)}) async-start(), calls=%async_computation.14 | async-start | bytes 1572864 | tf_op jit(solution)/shard_map/all_gather | solution.py:256
  498.1 67.3 %copy-start.74 = (f32[1024]{0:T(1024)S(1)}, f32[1024]{0:T(1024)}, u32[]{:S(2)}) copy-start(f32[1024]{0:T(1024)} %param.41) | copy-start | bytes 12292
  498.1 164.2 %all-reduce.42.cloned.1.call-start = ((), (), s32[]{:S(2)}) async-start(), calls=%async_computation.15 | async-start | bytes 4194304 | tf_op jit(solution)/shard_map/psum | solution.py:264
  586.1 7.0 copy-start.112
  599.2 664.4 %reduce-scatter.17.cloned.1.call-start = ((), (), s32[]{:S(2)}) async-start(), calls=%async_computation.13 | async-start | bytes 1572864 | tf_op jit(solution)/shard_map/reduce_scatter | solution.py:252
  613.5 652.5 %reduce-scatter.39.cloned.1.call-start = ((), (), s32[]{:S(2)}) async-start(), calls=%async_computation.26 | async-start | bytes 278528
  1139.5 127.8 %reduce-scatter.37.cloned.1.call-start = ((), (), s32[]{:S(2)}) async-start(), calls=%async_computation.25 | async-start | bytes 278528
  1140.9 173.6 %reduce-scatter.23.cloned.1.call-start = ((), (), s32[]{:S(2)}) async-start(), calls=%async_computation.18 | async-start | bytes 1114112 | tf_op jit(solution)/shard_map/reduce_scatter | solution.py:295
  1145.2 229.6 %reduce-scatter.21.cloned.1.call-start = ((), (), s32[]{:S(2)}) async-start(), calls=%async_computation.17 | async-start | bytes 1114112 | tf_op jit(solution)/shard_map/reduce_scatter | solution.py:292
  1149.7 293.3 %reduce-scatter.33.cloned.1.call-start = ((), (), s32[]{:S(2)}) async-start(), calls=%async_computation.23 | async-start | bytes 3063808 | tf_op jit(solution)/shard_map/reduce_scatter | solution.py:316
  1154.7 356.1 %reduce-scatter.31.cloned.1.call-start = ((), (), s32[]{:S(2)}) async-start(), calls=%async_computation.22 | async-start | bytes 3063808 | tf_op jit(solution)/shard_map/reduce_scatter | solution.py:313
  1159.6 419.3 %reduce-scatter.35.cloned.1.call-start = ((), (), s32[]{:S(2)}) async-start(), calls=%async_computation.24 | async-start | bytes 3063808 | tf_op jit(solution)/shard_map/reduce_scatter | solution.py:319
  1165.6 477.8 %reduce-scatter.29.cloned.1.call-start = ((), (), s32[]{:S(2)}) async-start(), calls=%async_computation.21 | async-start | bytes 2228224 | tf_op jit(solution)/shard_map/reduce_scatter | solution.py:310
  1171.1 536.8 %reduce-scatter.25.cloned.1.call-start = ((), (), s32[]{:S(2)}) async-start(), calls=%async_computation.19 | async-start | bytes 2228224 | tf_op jit(solution)/shard_map/reduce_scatter | solution.py:298
  1183.0 589.3 %reduce-scatter.27.cloned.1.call-start = ((), (), s32[]{:S(2)}) async-start(), calls=%async_computation.20 | async-start | bytes 2228224 | tf_op jit(solution)/shard_map/reduce_scatter | solution.py:301
  1187.0 618.2 %reduce-scatter.19.cloned.1.call-start = ((), (), s32[]{:S(2)}) async-start(), calls=%async_computation.16 | async-start | bytes 3145728 | tf_op jit(solution)/shard_map/reduce_scatter | solution.py:278
  1197.6 64.6 %copy-start.8 = (f32[512,1024]{1,0:T(8,128)S(1)}, f32[512,1024]{1,0:T(8,128)}, u32[]{:S(2)}) copy-start(f32[512,1024]{1,0:T(8,128)} %get-tuple-element.2407) | copy-start | bytes 6291460
  1805.3 44.5 %copy-start.1 = (bf16[1408,1024]{1,0:T(8,128)(2,1)S(1)}, bf16[1408,1024]{1,0:T(8,128)(2,1)}, u32[]{:S(2)}) copy-start(bf16[1408,1024]{1,0:T(8,128)(2,1)} %param.44) | copy-start | bytes 8650756
  (186 other events, 661.8 us)
Sparse Core Ops, SparseCore 0:
  497.5 65.6 all-reduce.39
  564.8 21.2 all-gather.1
  599.3 62.9 all-reduce.41
  664.4 20.3 reduce-scatter.16
  1139.6 55.8 reduce-scatter.38
  1199.5 54.7 reduce-scatter.36
  1257.9 56.5 reduce-scatter.22
  1318.1 56.6 reduce-scatter.20
  1378.6 64.2 reduce-scatter.32
  1446.6 64.2 reduce-scatter.30
  1514.6 64.2 reduce-scatter.34
  1582.5 60.9 reduce-scatter.28
  1647.2 60.7 reduce-scatter.24
  1711.5 60.7 reduce-scatter.26
  1774.4 30.8 reduce-scatter.18
where the time goes:
time: 1870 us; the launch traced here: 1860 us
  waiting for transfers between devices  648 us (35%)
  other arithmetic  523 us (28%)
  matrix products  366 us (20%)
  local copies, waits for them, and re-layouts  189 us (10%)
  blocking collectives  101 us (5%)
    another operation x64, other arithmetic, advance(): jax.scipy.linalg.solve_triangular(lower_part, target, lower=True, unit_di...  341 us
    reduce_scatter x1, waiting for transfers between devices, per_device(): lax.psum_scatter(upward_grad.astype(jnp.bfloat16), 'dp', scatter_dimensio...  66.6 us
    reduce_scatter x1, waiting for transfers between devices, per_device(): lax.psum_scatter(downward_grad.astype(jnp.bfloat16), 'dp', scatter_dimens...  66.4 us
    reduce_scatter x1, waiting for transfers between devices, per_device(): lax.psum_scatter(gating_grad.astype(jnp.bfloat16), 'dp', scatter_dimensio...  66.2 us
    psum x1, waiting for transfers between devices, per_device(): mixed_all = lax.psum(mixer_part, 'tensor')  64.8 us
    reduce_scatter x1, waiting for transfers between devices, per_device(): lax.psum_scatter(proj_grads[2].astype(jnp.bfloat16), 'dp', scatter_dimens...  62.9 us
    reduce_scatter x1, waiting for transfers between devices, per_device(): lax.psum_scatter(outward_grad.astype(jnp.bfloat16), 'dp', scatter_dimensi...  62.9 us
    reduce_scatter x1, waiting for transfers between devices, per_device(): lax.psum_scatter(proj_grads[3].astype(jnp.bfloat16), 'dp', scatter_dimens...  62.7 us
  transfers between devices with their start and end apart: 15, of which 12 were waited for; matrix products, arithmetic and copies ran while one was open for 31% of the time, Pallas kernels for 0%

commit v1 on v0

v1 whole, which is shorter than its diff:
```python
import functools

import jax
import jax.numpy as jnp
from jax import lax
from jax.experimental import pallas as pl
from jax.experimental.pallas import tpu as pltpu
from jax.sharding import PartitionSpec as P

CHUNK = 256
EPSILON = 1e-06
F32 = jnp.float32
BF16 = jnp.bfloat16

NN = (((1,), (0,)), ((), ()))
NT = (((1,), (1,)), ((), ()))
TN = (((0,), (0,)), ((), ()))


def split(value):
    high = value.astype(BF16)
    return high, (value - high.astype(F32)).astype(BF16)


def mm(left, right, dims):
    dot = functools.partial(lax.dot_general, dimension_numbers=dims, preferred_element_type=F32)
    return dot(left[0], right[0]) + (dot(left[0], right[1]) + dot(left[1], right[0]))


def iotas(rows, columns):
    return (
        lax.broadcasted_iota(jnp.int32, (rows, columns), 0),
        lax.broadcasted_iota(jnp.int32, (rows, columns), 1),
    )


def to_column(row, eye):
    return jnp.sum(jnp.where(eye, row, 0.0), axis=1, keepdims=True)


def to_row(column, eye):
    return jnp.sum(jnp.where(eye, column, 0.0), axis=0, keepdims=True)


def live_masks(segment_column, taps):
    length = segment_column.shape[0]
    wide = jnp.broadcast_to(segment_column, (length, 128))
    rows, _ = iotas(length, 128)
    masks = [None]
    for tap in range(1, taps):
        same = jnp.logical_and(pltpu.roll(wide, tap, 0) == wide, rows >= tap)
        masks.append(jnp.where(same, 1.0, 0.0))
    return masks


def widen(mask, width):
    return jnp.concatenate([mask] * (width // 128), axis=1) if width > 128 else mask


def conv_forward(pre, weight, masks):
    total = pre * weight[0:1]
    for tap in range(1, len(masks)):
        mask = widen(masks[tap], pre.shape[1])
        total = total + pltpu.roll(pre, tap, 0) * mask * weight[tap : tap + 1]
    return total


def conv_backward(upstream, pre, weight, masks):
    length = pre.shape[0]
    back = upstream * weight[0:1]
    weight_rows = [jnp.sum(upstream * pre, axis=0, keepdims=True)]
    for tap in range(1, len(masks)):
        masked = upstream * widen(masks[tap], pre.shape[1])
        back = back + pltpu.roll(masked, length - tap, 0) * weight[tap : tap + 1]
        weight_rows.append(jnp.sum(masked * pltpu.roll(pre, tap, 0), axis=0, keepdims=True))
    return back, jnp.concatenate(weight_rows, axis=0)


def slope(argument, logistic):
    return logistic * (1.0 + argument * (1.0 - logistic))


def unit_rows(values):
    return lax.rsqrt(jnp.sum(values * values, axis=1, keepdims=True) + EPSILON)


def chunk_decays(seg_row, cum_row, at, size, eye):
    rows, cols = iotas(size, size)
    seg = seg_row[:, at : at + size]
    cum = cum_row[:, at : at + size]
    seg_col, cum_col = to_column(seg, eye), to_column(cum, eye)
    keep = jnp.logical_and(rows >= cols, seg_col == seg)
    within = jnp.where(keep, jnp.exp(jnp.where(keep, cum_col - cum, 0.0)), 0.0)
    last_seg, last_cum = seg[:, size - 1 :], cum[:, size - 1 :]
    end = jnp.where(seg_col == last_seg, jnp.exp(last_cum - cum_col), 0.0)
    if at == 0:
        return within, end, None, None
    prev_seg = seg_row[:, at - 1 : at]
    start = jnp.where(seg_col == prev_seg, jnp.exp(cum_col), 0.0)
    carried = jnp.where(last_seg == prev_seg, jnp.exp(last_cum), 0.0)
    return within, end, start, carried


def invert_unit_lower(lower, size):
    rows, cols = iotas(size, size)
    inverse = jnp.where(rows == cols, 1.0, 0.0)
    shift = 0
    while (1 << shift) < size:
        pair = lax.shift_right_logical(rows, shift + 1) == lax.shift_right_logical(cols, shift + 1)
        odd = jnp.bitwise_and(lax.shift_right_logical(rows, shift), 1) == 1
        even = jnp.bitwise_and(lax.shift_right_logical(cols, shift), 1) == 0
        part = jnp.where(jnp.logical_and(pair, jnp.logical_and(odd, even)), lower, 0.0)
        if shift == 0:
            inverse = inverse - part
        else:
            both = split(inverse)
            inverse = inverse - mm(split(mm(both, split(part), NN)), both, NN)
        shift += 1
    return inverse


def forward_kernel(
    chunk, seg_ref, cum_ref, beta_ref, qp_ref, kp_ref, vp_ref, gp_ref, qw_ref, kw_ref, vw_ref,
    og_ref, gated_ref, rec_ref, upd_ref, inv_ref, mem_ref,
):
    length, key_dim = qp_ref.shape
    rows, cols = iotas(chunk, chunk)
    eye = rows == cols
    seg_row, cum_row, beta_row = seg_ref[...], cum_ref[0], beta_ref[0]
    seg_col = jnp.concatenate(
        [to_column(seg_row[:, at : at + chunk], eye) for at in range(0, length, chunk)], axis=0
    )
    masks = live_masks(seg_col, qw_ref.shape[0])

    def silu_conv(pre_ref, weight_ref):
        summed = conv_forward(pre_ref[...], weight_ref[...], masks)
        return summed * jax.nn.sigmoid(summed)

    queries = silu_conv(qp_ref, qw_ref)
    queries = queries * unit_rows(queries) * key_dim ** (-0.5)
    keys = silu_conv(kp_ref, kw_ref)
    keys = keys * unit_rows(keys)
    values = silu_conv(vp_ref, vw_ref)
    gain = og_ref[...]
    memory = None
    for at in range(0, length, chunk):
        here = slice(at, at + chunk)
        within, end, start, carried = chunk_decays(seg_row, cum_row, at, chunk, eye)
        beta = to_column(beta_row[:, here], eye)
        query, key = split(queries[here]), split(keys[here])
        lower = jnp.where(rows > cols, mm(key, key, NT) * within, 0.0) * beta
        inverse = invert_unit_lower(lower, chunk)
        target = values[here]
        if memory is not None:
            mem = split(memory)
            target = target - start * mm(key, mem, NN)
            mem_ref[0, at // chunk * key_dim : (at // chunk + 1) * key_dim, :] = memory
        else:
            mem_ref[0, 0:key_dim, :] = jnp.zeros_like(mem_ref[0, 0:key_dim, :])
        update = mm(split(inverse), split(beta * target), NN)
        upd = split(update)
        scores = mm(query, key, NT) * within
        output = mm(split(scores), upd, NN)
        if memory is not None:
            output = output + start * mm(query, mem, NN)
        if at + chunk < length:
            grown = mm(split(keys[here] * end), upd, TN)
            memory = grown if memory is None else carried * memory + grown
        factor = lax.rsqrt(jnp.mean(output * output, axis=1, keepdims=True) + EPSILON)
        gate = gp_ref[here, :]
        gated_ref[here, :] = (
            output * factor * gain * (gate * jax.nn.sigmoid(gate))
        ).astype(BF16)
        rec_ref[here, :] = output
        upd_ref[here, :] = update
        inv_ref[0, here, :] = inverse


def backward_kernel(
    chunk, seg_ref, cum_ref, beta_ref, qp_ref, kp_ref, vp_ref, gp_ref, qw_ref, kw_ref, vw_ref,
    og_ref, rec_ref, upd_ref, inv_ref, mem_ref, up_ref,
    dq_ref, dk_ref, dv_ref, dg_ref, dqw_ref, dkw_ref, dvw_ref, dog_ref, dbeta_ref, dcum_ref,
    query_scr, key_scr, value_scr,
):
    length, key_dim = qp_ref.shape
    scale = key_dim ** (-0.5)
    rows, cols = iotas(chunk, chunk)
    eye = rows == cols
    seg_row, cum_row, beta_row = seg_ref[...], cum_ref[0], beta_ref[0]
    seg_col = jnp.concatenate(
        [to_column(seg_row[:, at : at + chunk], eye) for at in range(0, length, chunk)], axis=0
    )
    masks = live_masks(seg_col, qw_ref.shape[0])
    query_sum = conv_forward(qp_ref[...], qw_ref[...], masks)
    key_sum = conv_forward(kp_ref[...], kw_ref[...], masks)
    value_sum = conv_forward(vp_ref[...], vw_ref[...], masks)
    query_sig, key_sig = jax.nn.sigmoid(query_sum), jax.nn.sigmoid(key_sum)
    value_sig = jax.nn.sigmoid(value_sum)
    query_act, key_act = query_sum * query_sig, key_sum * key_sig
    query_norm, key_norm = unit_rows(query_act), unit_rows(key_act)
    queries = query_act * query_norm * scale
    keys = key_act * key_norm
    values = value_sum * value_sig
    gain = og_ref[...]
    gain_grad = jnp.zeros_like(gain)
    grad_memory = None
    for at in reversed(range(0, length, chunk)):
        here = slice(at, at + chunk)
        index = at // chunk
        output, gate, up = rec_ref[here, :], gp_ref[here, :], up_ref[here, :]
        factor = lax.rsqrt(jnp.mean(output * output, axis=1, keepdims=True) + EPSILON)
        gate_sig = jax.nn.sigmoid(gate)
        normed = output * factor
        silu_gate = gate * gate_sig
        dg_ref[here, :] = (up * normed * gain * slope(gate, gate_sig)).astype(BF16)
        gain_grad = gain_grad + jnp.sum(up * normed * silu_gate, axis=0, keepdims=True)
        weighted = up * gain * silu_gate
        grad_out = factor * (
            weighted - normed * jnp.mean(weighted * normed, axis=1, keepdims=True)
        )
        within, end, start, carried = chunk_decays(seg_row, cum_row, at, chunk, eye)
        beta = to_column(beta_row[:, here], eye)
        query_f, key_f = queries[here], keys[here]
        query, key = split(query_f), split(key_f)
        update = upd_ref[here, :]
        upd = split(update)
        gram = jnp.where(rows > cols, mm(key, key, NT) * within, 0.0)
        scores = mm(query, key, NT) * within
        grad_o = split(grad_out)
        grad_update = mm(split(scores), grad_o, TN)
        if grad_memory is not None:
            grad_mem = split(grad_memory)
            grad_update = grad_update + mm(split(key_f * end), grad_mem, NN)
        grad_target = mm(split(inv_ref[0, here, :]), split(grad_update), TN)
        grad_scores = mm(grad_o, upd, NT)
        grad_lower = jnp.where(rows > cols, -mm(split(grad_target), upd, NT), 0.0)
        residual = values[here]
        grad_resid = beta * grad_target
        spread = grad_scores * scores + grad_lower * gram * beta
        cum_column = jnp.sum(spread, axis=1, keepdims=True)
        cum_line = -jnp.sum(spread, axis=0, keepdims=True)
        grad_prod = split(grad_scores * within)
        grad_gram = split(grad_lower * within * beta)
        grad_query = mm(grad_prod, key, NN)
        grad_key = mm(grad_prod, query, TN) + mm(grad_gram, key, NN) + mm(grad_gram, key, TN)
        new_grad_memory = None
        if at > 0:
            memory = mem_ref[0, index * key_dim : (index + 1) * key_dim, :]
            mem = split(memory)
            key_mem, query_mem = mm(key, mem, NN), mm(query, mem, NN)
            residual = residual - start * key_mem
            start_out, start_res = start * grad_out, start * grad_resid
            cum_column = cum_column + jnp.sum(
                start_out * query_mem - start_res * key_mem, axis=1, keepdims=True
            )
            start_o, start_r = split(start_out), split(start_res)
            grad_query = grad_query + mm(start_o, mem, NT)
            grad_key = grad_key - mm(start_r, mem, NT)
            new_grad_memory = mm(query, start_o, TN) - mm(key, start_r, TN)
        beta_grad = jnp.sum(grad_target * residual, axis=1, keepdims=True) + jnp.sum(
            grad_lower * gram, axis=1, keepdims=True
        )
        if grad_memory is not None:
            tail = end * mm(upd, grad_mem, NT)
            grad_key = grad_key + tail
            tail_rows = jnp.sum(tail * key_f, axis=1, keepdims=True)
            cum_column = cum_column - tail_rows
            last = jnp.sum(tail_rows, axis=0, keepdims=True)
            if at > 0:
                last = last + carried * jnp.sum(
                    jnp.sum(grad_memory * memory, axis=1, keepdims=True), axis=0, keepdims=True
                )
                new_grad_memory = new_grad_memory + carried * grad_memory
            cum_line = cum_line + jnp.where(cols[0:1] == chunk - 1, last, 0.0)
        grad_memory = new_grad_memory
        dcum_ref[0, :, here] = cum_line + to_row(cum_column, eye)
        dbeta_ref[0, :, here] = to_row(beta_grad, eye)
        query_scr[here, :] = grad_query
        key_scr[here, :] = grad_key
        value_scr[here, :] = grad_resid
    dog_ref[0] = gain_grad
    grad_query, grad_key = query_scr[...], key_scr[...]
    grad_query = (scale * query_norm) * (
        grad_query
        - query_act
        * (query_norm * query_norm * jnp.sum(grad_query * query_act, axis=1, keepdims=True))
    )
    grad_key = key_norm * (
        grad_key
        - key_act * (key_norm * key_norm * jnp.sum(grad_key * key_act, axis=1, keepdims=True))
    )
    back, dqw_ref[...] = conv_backward(
        grad_query * slope(query_sum, query_sig), qp_ref[...], qw_ref[...], masks
    )
    dq_ref[...] = back.astype(BF16)
    back, dkw_ref[...] = conv_backward(
        grad_key * slope(key_sum, key_sig), kp_ref[...], kw_ref[...], masks
    )
    dk_ref[...] = back.astype(BF16)
    back, dvw_ref[...] = conv_backward(
        value_scr[...] * slope(value_sum, value_sig), vp_ref[...], vw_ref[...], masks
    )
    dv_ref[...] = back.astype(BF16)


class Mixer:
    def __init__(self, length, heads, key_dim, value_dim, taps):
        self.chunk = min(CHUNK, length)
        self.length, self.heads = length, heads
        self.key_dim, self.value_dim, self.taps = key_dim, value_dim, taps
        chunks = length // self.chunk
        self.whole = pl.BlockSpec((1, length), lambda h: (0, 0))
        self.line = pl.BlockSpec((1, 1, length), lambda h: (h, 0, 0))
        self.narrow = pl.BlockSpec((length, key_dim), lambda h: (0, h))
        self.wide = pl.BlockSpec((length, value_dim), lambda h: (0, h))
        self.narrow_taps = pl.BlockSpec((taps, key_dim), lambda h: (0, h))
        self.wide_taps = pl.BlockSpec((taps, value_dim), lambda h: (0, h))
        self.gain = pl.BlockSpec((1, value_dim), lambda h: (0, 0))
        self.gain_out = pl.BlockSpec((1, 1, value_dim), lambda h: (h, 0, 0))
        self.inverse = pl.BlockSpec((1, length, self.chunk), lambda h: (h, 0, 0))
        self.memory = pl.BlockSpec((1, chunks * key_dim, value_dim), lambda h: (h, 0, 0))
        self.chunks = chunks
        self.inputs = (
            [self.whole] + [self.line] * 2 + [self.narrow] * 2 + [self.wide] * 2
            + [self.narrow_taps] * 2 + [self.wide_taps, self.gain]
        )
        self.params = pltpu.CompilerParams(
            dimension_semantics=("arbitrary",), vmem_limit_bytes=56 << 20
        )

    def cost(self, products):
        flops = 2 * self.heads * self.chunks * products * 3 * self.chunk**3
        return pl.CostEstimate(
            flops=flops,
            transcendentals=self.heads * self.length * 2048,
            bytes_accessed=self.heads * self.length * 1600 * 4,
        )

    def forward(self, *arguments):
        length, heads, values = self.length, self.heads, self.heads * self.value_dim
        return pl.pallas_call(
            functools.partial(forward_kernel, self.chunk),
            grid=(heads,),
            in_specs=self.inputs,
            out_specs=[self.wide] * 3 + [self.inverse, self.memory],
            out_shape=[
                jax.ShapeDtypeStruct((length, values), BF16),
                jax.ShapeDtypeStruct((length, values), F32),
                jax.ShapeDtypeStruct((length, values), F32),
                jax.ShapeDtypeStruct((heads, length, self.chunk), F32),
                jax.ShapeDtypeStruct((heads, self.chunks * self.key_dim, self.value_dim), F32),
            ],
            compiler_params=self.params,
            cost_estimate=self.cost(20),
            name="mixer_forward",
        )(*arguments)

    def backward(self, *arguments):
        length, heads = self.length, self.heads
        keys, values = heads * self.key_dim, heads * self.value_dim
        return pl.pallas_call(
            functools.partial(backward_kernel, self.chunk),
            grid=(heads,),
            in_specs=self.inputs + [self.wide] * 2 + [self.inverse, self.memory, self.wide],
            out_specs=[self.narrow] * 2 + [self.wide] * 2 + [self.narrow_taps] * 2
            + [self.wide_taps, self.gain_out] + [self.line] * 2,
            out_shape=[
                jax.ShapeDtypeStruct((length, keys), BF16),
                jax.ShapeDtypeStruct((length, keys), BF16),
                jax.ShapeDtypeStruct((length, values), BF16),
                jax.ShapeDtypeStruct((length, values), BF16),
                jax.ShapeDtypeStruct((self.taps, keys), F32),
                jax.ShapeDtypeStruct((self.taps, keys), F32),
                jax.ShapeDtypeStruct((self.taps, values), F32),
                jax.ShapeDtypeStruct((heads, 1, self.value_dim), F32),
                jax.ShapeDtypeStruct((heads, 1, length), F32),
                jax.ShapeDtypeStruct((heads, 1, length), F32),
            ],
            scratch_shapes=[
                pltpu.VMEM((length, self.key_dim), F32),
                pltpu.VMEM((length, self.key_dim), F32),
                pltpu.VMEM((length, self.value_dim), F32),
            ],
            compiler_params=self.params,
            cost_estimate=self.cost(14),
            name="mixer_backward",
        )(*arguments)


def swapped(value, axis, bit):
    count = lax.axis_size(axis)
    return lax.ppermute(value, axis, [(i, i ^ (1 << bit)) for i in range(count)])


def axis_bits(axis):
    count = lax.axis_size(axis)
    bits = count.bit_length() - 1
    assert count == 1 << bits, "axis size"
    return bits


def scatter_rows(value, axis, order):
    bits = axis_bits(axis)
    index = lax.axis_index(axis)
    rows = value.shape[0] >> bits
    value = value.reshape((2,) * bits + (rows,) + value.shape[1:])
    left = list(range(bits - 1, -1, -1))
    for step, bit in enumerate(order):
        dim = left.index(bit)
        mine = jnp.bitwise_and(lax.shift_right_logical(index, bit), 1)
        keep = lax.dynamic_index_in_dim(value, mine, dim, keepdims=False)
        send = lax.dynamic_index_in_dim(value, 1 - mine, dim, keepdims=False)
        value = keep.astype(F32) + swapped(send, axis, bit).astype(F32)
        if step + 1 < bits:
            value = value.astype(BF16)
        left.pop(dim)
    return value


def all_sum(value, axis):
    for bit in range(axis_bits(axis)):
        value = value + swapped(value, axis, bit)
    return value


def all_sum_low(value, axis):
    for bit in range(axis_bits(axis)):
        low = value.astype(BF16)
        value = low.astype(F32) + swapped(low, axis, bit).astype(F32)
    return value


def dot(left, right, dims=NN, out=F32):
    return lax.dot_general(left, right, dims, preferred_element_type=out)


def per_device(
    tokens, segment_ids, mixer_gain, query_weight, key_weight, value_weight, gate_weight,
    beta_weight, decay_weight, query_conv, key_conv, value_conv, decay_log, decay_bias,
    output_gain, out_weight, feed_gain, feed_gate, feed_up, feed_down, cotangent,
):
    seq_count, length = segment_ids.shape
    assert seq_count == 1
    heads, value_dim = decay_log.shape[0], output_gain.shape[0]
    key_dim = query_weight.shape[1] // heads
    tensor_bits = axis_bits("tensor")
    tensor_order = list(range(tensor_bits - 1, -1, -1))
    share = length >> tensor_bits
    first_row = lax.axis_index("tensor") * share

    def my_rows(value):
        return lax.dynamic_slice_in_dim(value, first_row, share, 0)

    mixer = Mixer(length, heads, key_dim, value_dim, query_conv.shape[0])
    chunk = mixer.chunk
    cotangent_all = lax.all_gather(cotangent, "tensor", axis=0, tiled=True)
    inputs = tokens.astype(F32)
    factor_first = lax.rsqrt(jnp.mean(inputs * inputs, axis=-1, keepdims=True) + EPSILON)
    normed_in = (inputs * factor_first * mixer_gain).astype(BF16)
    query_pre, key_pre = dot(normed_in, query_weight), dot(normed_in, key_weight)
    value_pre, gate_pre = dot(normed_in, value_weight), dot(normed_in, gate_weight)
    small_weight = jnp.concatenate([beta_weight, decay_weight], axis=1)
    small_pre = dot(small_weight, normed_in, (((0,), (1,)), ((), ())))

    def rates(small, log, bias):
        beta = jax.nn.sigmoid(small[:heads])
        log_decay = -jnp.exp(log)[:, None] * jax.nn.softplus(small[heads:] + bias[:, None])
        summed = jnp.cumsum(log_decay.reshape(heads, length // chunk, chunk), axis=-1)
        return summed.reshape(heads, 1, length), beta.reshape(heads, 1, length)

    (cum, beta), rates_back = jax.vjp(rates, small_pre, decay_log, decay_bias)
    shared = (
        segment_ids.astype(F32), cum, beta, query_pre, key_pre, value_pre, gate_pre,
        query_conv, key_conv, value_conv, output_gain[None],
    )
    gated, recurrent, update, inverse, memory = mixer.forward(*shared)
    middle = inputs + all_sum_low(dot(gated, out_weight), "tensor")
    factor_second = lax.rsqrt(jnp.mean(middle * middle, axis=-1, keepdims=True) + EPSILON)
    normed_mid = (middle * factor_second * feed_gain).astype(BF16)
    swish_in, linear_up = dot(normed_mid, feed_gate), dot(normed_mid, feed_up)
    grad_hidden = dot(cotangent_all, feed_down, NT)
    logistic = jax.nn.sigmoid(swish_in)
    swish = swish_in * logistic
    hidden = (swish * linear_up).astype(BF16)
    swish_grad = (grad_hidden * linear_up * slope(swish_in, logistic)).astype(BF16)
    linear_grad = (grad_hidden * swish).astype(BF16)
    second_part = dot(swish_grad, feed_gate, NT) + dot(linear_grad, feed_up, NT)
    grad_second = all_sum_low(second_part, "tensor")
    feed_part = dot(hidden, feed_down, out=BF16)
    feed_rows = scatter_rows(feed_part, "tensor", tensor_order)
    block_out = (my_rows(middle) + feed_rows).astype(BF16)

    def norm_backward(upstream, values, factor, gain):
        unit = values * factor
        weighted = upstream * gain
        mean = jnp.mean(weighted * unit, axis=-1, keepdims=True)
        return factor * (weighted - unit * mean), upstream * unit

    dp_bits = axis_bits("dp")
    across = [0] + [bit for bit in (1, 2, 3) if bit < dp_bits] + list(range(4, dp_bits))
    along = [0] + list(range(2, dp_bits)) + ([1] if dp_bits > 1 else [])
    if dp_bits == 0:
        across = along = []
    gate_sum = scatter_rows(dot(normed_mid, swish_grad, TN, BF16), "dp", across)
    up_sum = scatter_rows(dot(normed_mid, linear_grad, TN, BF16), "dp", along)
    down_sum = scatter_rows(dot(cotangent_all, hidden, TN, BF16), "dp", across)

    back_second, second_terms = norm_backward(grad_second, middle, factor_second, feed_gain)
    gain_second = jnp.sum(my_rows(second_terms), axis=0)
    grad_middle = cotangent_all.astype(F32) + back_second
    grad_middle_low = grad_middle.astype(BF16)
    grad_gated = dot(grad_middle_low, out_weight, NT)
    out_sum = scatter_rows(dot(grad_middle_low, gated, TN, BF16), "dp", along)

    (
        low_query, low_key, low_value, low_gate, query_taps, key_taps, value_taps, gain_heads,
        beta_rows, cum_rows,
    ) = mixer.backward(*shared, recurrent, update, inverse, memory, grad_gated)
    small_grad, log_grad, bias_grad = rates_back((cum_rows, beta_rows))
    low_small = small_grad.astype(BF16)
    first_part = (
        dot(low_query, query_weight, NT)
        + dot(low_key, key_weight, NT)
        + dot(low_value, value_weight, NT)
        + dot(low_gate, gate_weight, NT)
        + dot(low_small, small_weight, (((0,), (1,)), ((), ())))
    )
    grad_first = scatter_rows(first_part.astype(BF16), "tensor", tensor_order)
    value_sum = scatter_rows(dot(normed_in, low_value, TN, BF16), "dp", across)
    gate_proj_sum = scatter_rows(dot(normed_in, low_gate, TN, BF16), "dp", along)
    query_sum = scatter_rows(dot(normed_in, low_query, TN, BF16), "dp", across)
    key_sum = scatter_rows(dot(normed_in, low_key, TN, BF16), "dp", along)
    small_sum = scatter_rows(
        dot(normed_in, low_small, (((0,), (1,)), ((), ())), BF16), "dp", across
    )
    back_first, first_terms = norm_backward(
        grad_first, my_rows(inputs), my_rows(factor_first), mixer_gain
    )
    tokens_grad = (my_rows(grad_middle) + back_first).astype(BF16)

    gains = [jnp.sum(first_terms, axis=0), gain_second, jnp.sum(gain_heads, axis=(0, 1))]
    taps = [query_taps.reshape(-1), key_taps.reshape(-1), value_taps.reshape(-1)]
    own = taps + [log_grad, bias_grad]
    gains_sum = all_sum(jnp.concatenate(gains), "tensor")
    packed = all_sum(jnp.concatenate([gains_sum] + own), "dp")
    sums, place = [], 0
    for piece in gains + own:
        sums.append(packed[place : place + piece.shape[0]])
        place += piece.shape[0]
    return (
        block_out,
        tokens_grad,
        sums[0],
        query_sum,
        key_sum,
        value_sum,
        gate_proj_sum,
        small_sum[:, :heads],
        small_sum[:, heads:],
        sums[3].reshape(query_conv.shape),
        sums[4].reshape(key_conv.shape),
        sums[5].reshape(value_conv.shape),
        sums[6],
        sums[7],
        sums[2],
        out_sum.T,
        sums[1],
        gate_sum,
        up_sum,
        down_sum.T,
    )


def solution(mesh):
    rows, both = P("dp", None), P(("dp", "tensor"), None)
    columns, grid = P(None, "tensor"), P("dp", "tensor")
    in_specs = (
        (rows, rows, P())
        + (columns,) * 9
        + (P("tensor"), P("tensor"), P(), P("tensor", None), P())
        + (columns, columns, P("tensor", None), both)
    )
    out_specs = (
        (both, both, P())
        + (grid,) * 6
        + (columns,) * 3
        + (P("tensor"), P("tensor"), P(), P("tensor", "dp"), P())
        + (grid, grid, P("tensor", "dp"))
    )
    return jax.shard_map(
        per_device, mesh=mesh, in_specs=in_specs, out_specs=out_specs, check_vma=False
    )
```

time: 1870 us -> 460 us (0.25)
  waiting for transfers between devices: 648 us -> 152 us
  other arithmetic: 523 us -> 55.8 us
  matrix products: 366 us -> 75.1 us
  local copies, waits for them, and re-layouts: 189 us -> 35.3 us
  blocking collectives: 101 us -> 0 us
  Pallas kernels: 0 us -> 71.5 us
  starting transfers between devices: 1.3 us -> 47 us
    reduce_scatter x10 -> x0, waiting for transfers between devices: 524 us -> none  [the longest x1 66.6 us: per_device(): lax.psum_scatter(upward_grad.astype(jnp.bfloat16), 'dp', scatter_dimensio...]
    another operation x102 -> x6, other arithmetic: 346 us -> 13.6 us  [the longest x64 341 us: advance(): jax.scipy.linalg.solve_triangular(lower_part, target, lower=True, unit_di...]
    dot_general x182 -> x27, matrix products: 341 us -> 75.1 us  [dot(): return lax.dot_general(left, right, dims, preferred_element_type=out)]
    ppermute x0 -> x45, waiting for transfers between devices: none -> 152 us  [swapped(): return lax.ppermute(value, axis, [(i, i ^ 1 << bit) for i in range(count)])]
    psum x2 -> x0, waiting for transfers between devices: 114 us -> none  [the longest x1 64.8 us: per_device(): mixed_all = lax.psum(mixer_part, 'tensor')]
    psum x2 -> x0, blocking collectives: 101 us -> none  [the longest x1 61.5 us: per_device(): lax.psum((mixer_grads[6], mixer_grads[7], mixer_grads[8], mixer_grads[9],...]
    pallas_call x0 -> x2, Pallas kernels: none -> 71.5 us  [the longest x1 42.8 us: forward(): pl.pallas_call(functools.partial(forward_kernel, self.chunk), grid=(heads...]
    reduce_sum x53 -> x6, other arithmetic: 57.7 us -> 5.8 us  [the longest x1 2.4 us: per_device(): jnp.mean(middle * middle, axis=-1, keepdims=True) + EPSILON]
  transfers between devices with their start and end apart: 15 -> 46, of which waited for: 12 -> 23; matrix products, arithmetic and copies ran while one was open for 31% -> 27% of each run, Pallas kernels for 0% -> 6%
where the time goes in v1:
time: 460 us; the launch traced here: 452 us
  waiting for transfers between devices  152 us (33%)
  matrix products  75.1 us (16%)
  Pallas kernels  71.5 us (16%)
  other arithmetic  55.8 us (12%)
  starting transfers between devices  47 us (10%)
  local copies, waits for them, and re-layouts  35.3 us (8%)
  between operations  15.5 us (3%)
    ppermute x45, waiting for transfers between devices, swapped(): return lax.ppermute(value, axis, [(i, i ^ 1 << bit) for i in range(count)])  152 us
    dot_general x27, matrix products, dot(): return lax.dot_general(left, right, dims, preferred_element_type=out)  75.1 us
    ppermute x45, starting transfers between devices, swapped(): return lax.ppermute(value, axis, [(i, i ^ 1 << bit) for i in range(count)])  47 us
    pallas_call x1, Pallas kernels, forward(): pl.pallas_call(functools.partial(forward_kernel, self.chunk), grid=(heads...  42.8 us
    pallas_call x1, Pallas kernels, backward(): pl.pallas_call(functools.partial(backward_kernel, self.chunk), grid=(head...  28.7 us
    convert_element_type x27, other arithmetic, scatter_rows(): value = value.astype(BF16)  16.1 us
    another operation x6, other arithmetic  13.6 us
    dynamic_slice x6, local copies, waits for them, and re-layouts, scatter_rows(): keep = lax.dynamic_index_in_dim(value, mine, dim, keepdims=False)  10.8 us
  transfers between devices with their start and end apart: 46, of which 23 were waited for; matrix products, arithmetic and copies ran while one was open for 27% of the time, Pallas kernels for 6%

profile of v1, /device:TPU:0, one launch (start us, length us, event | category | flops | bytes accessed | tf_op | source)
XLA Modules:
  0.0 452.0 jit_solution(13134037213173683332)
XLA Ops:
  13.9 2.4 reduce-window.14
  17.9 3.3 fusion.64.qp_ref
  22.9 2.6 fusion.66.vp_ref
  25.5 2.6 fusion.67.gp_ref
  28.1 42.8 %mixer_forward.1 = (bf16[512,1024]{1,0:T(8,128)(2,1)}, f32[512,1024]{1,0:T(8,128)}, f32[512,1024]{1,0:T(8,128)}, f32[4,512,256]{2,1,0:T(8,128)}, f32[4,256,256]{2,1,0:T(8,128)}) custom-call(f32[1,512]{1,0:T(1,128)} %convert_element_type.481.seg_ref, f32[4,1,512]{2,1,0:T(1,128)} %bitcast.330, f32[4,1,512]{2,1,0:T(1,128)} %reshape.271.beta_ref, ...), custom_call_target="tpu_custom_call" | custom-call | flops 16106127360 | bytes 13107200 | tf_op jit(solution)/shard_map/mixer_forward/pallas_call | solution.py:341
  71.0 3.5 convolution_convert_fusion
  74.5 3.0 collective-permute-start
  77.5 2.8 convert_element_type.480
  80.4 31.8 %collective-permute-done = bf16[512,1024]{1,0:T(8,128)(2,1)} collective-permute-done((bf16[512,1024]{1,0:T(8,128)(2,1)}, bf16[512,1024]{1,0:T(8,128)(2,1)}, u32[]{:S(2)}, u32[]{:S(2)}) %collective-permute-start) | collective-permute-done | bytes 1048608 | tf_op jit(solution)/shard_map/ppermute | solution.py:392
  112.2 2.4 multiply_reduce_fusion.1
  118.3 3.4 fusion.68
  121.7 4.1 fusion.70
  125.8 2.9 multiply_convert_fusion
  128.7 1.8 fusion.71
  130.5 1.9 fusion.80
  132.4 1.8 fusion.69
  134.2 1.8 collective-permute-start.1
  136.0 11.6 %fusion.81 = bf16[1024,1408]{1,0:T(8,128)(2,1)S(1)} fusion(bf16[512,1024]{1,0:T(8,128)(2,1)S(1)} %copy-done.39, bf16[512,1408]{1,0:T(8,128)(2,1)S(1)} %get-tuple-element.58), kind=kOutput, calls=%fused_computation.227 | convolution fusion | flops 1476395008 | bytes 5373952 | tf_op jit(solution)/shard_map/dot_general | solution.py:434
  147.6 1.8 add_convert_fusion.1
  152.8 1.9 fusion.82
  154.7 2.1 constant_dynamic-slice_fusion.1
  161.2 12.1 %collective-permute-done.2 = bf16[512,1024]{1,0:T(8,128)(2,1)S(1)} collective-permute-done((bf16[512,1024]{1,0:T(8,128)(2,1)S(1)}, bf16[512,1024]{1,0:T(8,128)(2,1)S(1)}, u32[]{:S(2)}, u32[]{:S(2)}) %collective-permute-start.2) | collective-permute-done | bytes 1048608 | tf_op jit(solution)/shard_map/ppermute | solution.py:392
  173.3 1.8 convert_add_fusion.6
  176.7 2.6 fusion.29.up_ref
  179.3 28.7 %mixer_backward.1 = (bf16[512,512]{1,0:T(8,128)(2,1)}, bf16[512,512]{1,0:T(8,128)(2,1)}, bf16[512,1024]{1,0:T(8,128)(2,1)}, bf16[512,1024]{1,0:T(8,128)(2,1)}, f...) custom-call(f32[1,512]{1,0:T(1,128)} %convert_element_type.481.seg_r, ...), custom_call_target="tpu_custom_call" | custom-call | flops 11274289152 | bytes 13107200 | tf_op jit(solution)/shard_map/mixer_backward/pallas_call | solution.py:361
  208.0 3.2 fusion.73
  211.3 1.7 fusion.77
  213.0 2.1 fusion.72
  215.1 1.7 fusion.76
  217.3 2.6 fusion.74
  219.9 2.7 fusion.78
  222.6 2.6 fusion.27
  225.2 2.6 fusion.75
  227.9 2.6 fusion.79
  230.5 10.3 %reduce-window.16 = f32[4,2,2,128]{3,2,1,0:T(2,128)S(1)} reduce-window(f32[4,2,2,128]{3,2,1,0:T(2,128)S(1)} %bitcast.334, f32[]{:T(128)} %constant.235.clone.1), window={size=1x1x1x128 pad=0_0x0_0x0_0x0_127}, to_apply=%region_5.6 | reduce-window | flops 260096 | bytes 16388 | tf_op jit(solution)/shard_map/reduce-window.2
  242.9 4.0 add_convert_fusion
  249.6 4.6 %constant_dynamic-slice_fusion.7 = (bf16[2,2,2,1,64,1024]{5,4,3,2,1,0:T(8,128)(2,1)}, bf16[2,2,2,1,64,1024]{5,4,3,2,1,0:T(8,128)(2,1)}, bf16[2,2,2,1,64,1024]{5,...) fusion(bf16[2,2,2,2,64,1024]{5,4,3,2,1,0:T(8,128)(2,1)} %bitcast.313, s32[]{:T(128)S(6)} %select_n.144, ...), kind=kLoop, calls=%fused_computation.144 | loop fusion | bytes 8388616 | tf_op jit(solution)/shard_map/jit(dynamic_index_in_dim)/dynamic_slice | solution.py:411
  261.2 1.9 collective-permute-done.27
  263.2 2.6 collective-permute-start.28
  271.6 1.8 fusion.2
  273.5 2.1 fusion.1
  275.9 2.0 fusion
  290.5 2.6 add_convert_fusion.2
  293.2 8.8 %collective-permute-done.6 = f32[10504]{0:T(1024)S(1)} collective-permute-done((f32[10504]{0:T(1024)S(1)}, f32[10504]{0:T(1024)S(1)}, u32[]{:S(2)}, u32[]{:S(2)}) %collective-permute-start.6) | collective-permute-done | bytes 42048 | tf_op jit(solution)/shard_map/ppermute | solution.py:392
  303.7 2.4 collective-permute-done.7
  306.6 4.5 collective-permute-done.8
  319.3 6.0 %collective-permute-done.14 = bf16[2,2,64,512]{3,2,1,0:T(8,128)(2,1)S(1)} collective-permute-done((bf16[2,2,64,512]{3,2,1,0:T(8,128)(2,1)S(1)}, bf16[2,2,64,512]{3,2,1,0:T(8,128)(2,1)S(1)}, u32[]{:S(2)}, u32[]{:S(2)}) %collective-permute-start.14) | collective-permute-done | bytes 262176 | tf_op jit(solution)/shard_map/ppermute | solution.py:392
  327.1 3.6 collective-permute-done.11
  332.0 6.4 %collective-permute-done.15 = bf16[2,64,512]{2,1,0:T(8,128)(2,1)S(1)} collective-permute-done((bf16[2,64,512]{2,1,0:T(8,128)(2,1)S(1)}, bf16[2,64,512]{2,1,0:T(8,128)(2,1)S(1)}, u32[]{:S(2)}, u32[]{:S(2)}) %collective-permute-start.15) | collective-permute-done | bytes 131104 | tf_op jit(solution)/shard_map/ppermute | solution.py:392
  338.4 5.3 %collective-permute-done.12 = bf16[64,512]{1,0:T(8,128)(2,1)S(1)} collective-permute-done((bf16[64,512]{1,0:T(8,128)(2,1)S(1)}, bf16[64,512]{1,0:T(8,128)(2,1)S(1)}, u32[]{:S(2)}, u32[]{:S(2)}) %collective-permute-start.12) | collective-permute-done | bytes 65568 | tf_op jit(solution)/shard_map/ppermute | solution.py:392
  345.9 2.8 collective-permute-done.16
  355.1 2.1 collective-permute-start.22
  357.2 1.7 fusion.4
  360.5 11.3 %collective-permute-done.38 = bf16[2,2,64,1408]{3,2,1,0:T(8,128)(2,1)S(1)} collective-permute-done((bf16[2,2,64,1408]{3,2,1,0:T(8,128)(2,1)}, bf16[2,2,64,1408]{3,2,1,0:T(8,128)(2,1)S(1)}, u32[]{:S(2)}, u32[]{:S(2)}) %collective-permute-start.38) | collective-permute-done | bytes 720928 | tf_op jit(solution)/shard_map/ppermute | solution.py:392
  372.1 2.5 collective-permute-start.39
  374.8 25.3 %collective-permute-done.35 = bf16[2,64,1408]{2,1,0:T(8,128)(2,1)S(1)} collective-permute-done((bf16[2,64,1408]{2,1,0:T(8,128)(2,1)S(1)}, bf16[2,64,1408]{2,1,0:T(8,128)(2,1)S(1)}, u32[]{:S(2)}, u32[]{:S(2)}) %collective-permute-start.35) | collective-permute-done | bytes 360480 | tf_op jit(solution)/shard_map/ppermute | solution.py:392
  401.4 3.4 collective-permute-start.36
  404.9 8.9 %collective-permute-done.43 = bf16[2,64,1408]{2,1,0:T(8,128)(2,1)S(1)} collective-permute-done((bf16[2,64,1408]{2,1,0:T(8,128)(2,1)S(1)}, bf16[2,64,1408]{2,1,0:T(8,128)(2,1)S(1)}, u32[]{:S(2)}, u32[]{:S(2)}) %collective-permute-start.43) | collective-permute-done | bytes 360480 | tf_op jit(solution)/shard_map/ppermute | solution.py:392
  416.1 2.5 collective-permute-start.19
  419.2 3.0 collective-permute-start.31
  423.7 7.1 %collective-permute-done.44 = bf16[64,1408]{1,0:T(8,128)(2,1)S(1)} collective-permute-done((bf16[64,1408]{1,0:T(8,128)(2,1)S(1)}, bf16[64,1408]{1,0:T(8,128)(2,1)S(1)}, u32[]{:S(2)}, u32[]{:S(2)}) %collective-permute-start.44) | collective-permute-done | bytes 180256 | tf_op jit(solution)/shard_map/ppermute | solution.py:392
  431.8 2.8 collective-permute-done.23
  436.2 2.6 collective-permute-done.31
  441.9 2.0 collective-permute-done.32
  (330 shorter events, 90.0 us)
Async XLA Ops:
  7.2 118.6 %copy-start = (bf16[1024,1408]{1,0:T(8,128)(2,1)S(1)}, bf16[1024,1408]{1,0:T(8,128)(2,1)}, u32[]{:S(2)}) copy-start(bf16[1024,1408]{1,0:T(8,128)(2,1)} %param.38) | copy-start | bytes 8650756
  7.2 114.4 %all-gather.2.cloned.1.call-start = ((), (), s32[]{:S(2)}) async-start(), calls=%async_computation | async-start | bytes 1572864 | tf_op jit(solution)/shard_map/all_gather | solution.py:456
  28.1 42.9 %copy-start.56 = (bf16[1024,1024]{1,0:T(8,128)(2,1)S(1)}, bf16[1024,1024]{1,0:T(8,128)(2,1)}, u32[]{:S(2)}) copy-start(bf16[1024,1024]{1,0:T(8,128)(2,1)} %param.36) | copy-start | bytes 6291460
  74.5 37.7 %collective-permute-start = (bf16[512,1024]{1,0:T(8,128)(2,1)}, bf16[512,1024]{1,0:T(8,128)(2,1)}, u32[]{:S(2)}, u32[]{:S(2)}) collective-permute-start(bf16[512,1024]{1,0:T(8,128)(2,1)} %convolution_convert_fusion), channel_id=1, source_target_pairs={{0,1},{1,0},{2,3},{3,2},{4,5},{5,4},{6,7},{7,6},{8,9},{9,8},{10,11... | collective-permute-start | bytes 3145736 | tf_op jit(solution)/shard_map/ppermute | solution.py:392
  80.4 34.2 %copy-start.43 = (f32[1024]{0:T(1024)S(1)}, f32[1024]{0:T(1024)}, u32[]{:S(2)}) copy-start(f32[1024]{0:T(1024)} %param.37) | copy-start | bytes 12292
  134.2 25.6 %collective-permute-start.1 = (bf16[256,1024]{1,0:T(8,128)(2,1)S(1)}, bf16[256,1024]{1,0:T(8,128)(2,1)S(1)}, u32[]{:S(2)}, u32[]{:S(2)}) collective-permute-start(bf16[256,1024]{1,0:T(8,128)(2,1)S(1)} %dynamic-slice_bitcast_fusion.7), channel_id=1, source_target_pairs={{0,1},{1,0},{2,3},{3,2},{4,5},{5,4},{6,7},{7,6},{8,9},{9,8},{10,11... | collective-permute-start | bytes 1572872 | tf_op jit(solution)/shard_map/ppermute | solution.py:392
  136.0 11.6 %copy-start.55 = (bf16[1024,1408]{1,0:T(8,128)(2,1)S(1)}, bf16[1024,1408]{1,0:T(8,128)(2,1)}, u32[]{:S(2)}) copy-start(bf16[1024,1408]{1,0:T(8,128)(2,1)} %param.39) | copy-start | bytes 8650756
  149.4 23.8 %collective-permute-start.2 = (bf16[512,1024]{1,0:T(8,128)(2,1)S(1)}, bf16[512,1024]{1,0:T(8,128)(2,1)S(1)}, u32[]{:S(2)}, u32[]{:S(2)}) collective-permute-start(bf16[512,1024]{1,0:T(8,128)(2,1)S(1)} %add_convert_fusion.1), channel_id=1, source_target_pairs={{0,1},{1,0},{2,3},{3,2},{4,5},{5,4},{6,7},{7,6},{8,9},{9,8},{10,11... | collective-permute-start | bytes 3145736 | tf_op jit(solution)/shard_map/ppermute | solution.py:392
  152.4 118.7 %collective-permute-start.33 = (bf16[2,2,2,64,1408]{4,3,0,1,2:T(8,128)(2,1)}, bf16[2,2,2,64,1408]{4,3,0,1,2:T(8,128)(2,1)}, u32[]{:S(2)}, u32[]{:S(2)}) collective-permute-start(bf16[2,2,2,64,1408]{4,3,0,1,2:T(8,128)(2,1)} %bitcast.298), channel_id=1, source_target_pairs={{0,2},{2,0},{4,6},{6,4},{8,10},{10,8},{12,14},{14,12},{16,18},{18,... | collective-permute-start | bytes 4325384 | tf_op jit(solution)/shard_map/ppermute | solution.py:392
  158.0 115.4 %collective-permute-start.37 = (bf16[2,2,2,64,1408]{4,3,2,0,1:T(8,128)(2,1)}, bf16[2,2,2,64,1408]{4,3,2,0,1:T(8,128)(2,1)}, u32[]{:S(2)}, u32[]{:S(2)}) collective-permute-start(bf16[2,2,2,64,1408]{4,3,2,0,1:T(8,128)(2,1)} %bitcast.297), channel_id=1, source_target_pairs={{0,2},{2,0},{4,6},{6,4},{8,10},{10,8},{12,14},{14,12},{16,18},{18,... | collective-permute-start | bytes 4325384 | tf_op jit(solution)/shard_map/ppermute | solution.py:392
  158.1 15.2 %copy-start.2 = (f32[512,1024]{1,0:T(8,128)S(1)}, f32[512,1024]{1,0:T(8,128)}, u32[]{:S(2)}) copy-start(f32[512,1024]{1,0:T(8,128)} %get-tuple-element.55) | copy-start | bytes 6291460
  159.4 116.3 %collective-permute-start.41 = (bf16[2,2,2,64,1408]{4,3,0,1,2:T(8,128)(2,1)}, bf16[2,2,2,64,1408]{4,3,0,1,2:T(8,128)(2,1)}, u32[]{:S(2)}, u32[]{:S(2)}) collective-permute-start(bf16[2,2,2,64,1408]{4,3,0,1,2:T(8,128)(2,1)} %bitcast.296), channel_id=1, source_target_pairs={{0,2},{2,0},{4,6},{6,4},{8,10},{10,8},{12,14},{14,12},{16,18},{18,... | collective-permute-start | bytes 4325384 | tf_op jit(solution)/shard_map/ppermute | solution.py:392
  176.7 45.9 %copy-start.21 = (f32[512,1024]{1,0:T(8,128)}, f32[512,1024]{1,0:T(8,128)S(1)}, u32[]{:S(2)}) copy-start(f32[512,1024]{1,0:T(8,128)S(1)} %multiply_add_fusion) | copy-start | bytes 6291460
  179.3 28.7 %copy-start.33 = (bf16[1024,512]{1,0:T(8,128)(2,1)S(1)}, bf16[1024,512]{1,0:T(8,128)(2,1)}, u32[]{:S(2)}) copy-start(bf16[1024,512]{1,0:T(8,128)(2,1)} %param.25) | copy-start | bytes 3145732
  227.9 13.3 %copy-start.47 = (f32[4,1,512]{2,1,0:T(1,128)S(1)}, f32[4,1,512]{2,1,0:T(1,128)}, u32[]{:S(2)}) copy-start(f32[4,1,512]{2,1,0:T(1,128)} %get-tuple-element.45) | copy-start | bytes 24580
  248.7 32.0 %collective-permute-start.3 = (bf16[256,1024]{1,0:T(8,128)(2,1)}, bf16[256,1024]{1,0:T(8,128)(2,1)}, u32[]{:S(2)}, u32[]{:S(2)}) collective-permute-start(bf16[256,1024]{1,0:T(8,128)(2,1)} %dynamic-slice_bitcast_fusion.6), channel_id=1, source_target_pairs={{0,1},{1,0},{2,3},{3,2},{4,5},{5,4},{6,7},{7,6},{8,9},{9,8},{10,11... | collective-permute-start | bytes 1572872 | tf_op jit(solution)/shard_map/ppermute | solution.py:392
  249.5 6.2 %collective-permute-start.25 = (bf16[2,2,2,64,8]{3,4,0,1,2:T(8,128)(2,1)S(1)}, bf16[2,2,2,64,8]{3,4,0,1,2:T(8,128)(2,1)S(1)}, u32[]{:S(2)}, u32[]{:S(2)}) collective-permute-start(bf16[2,2,2,64,8]{3,4,0,1,2:T(8,128)(2,1)S(1)} %bitcast.326), channel_id=1, source_target_pairs={{0,2},{2,0},{4,6},{6,4},{8,10},{10,8},{12,14},{14,12},{16,18},{18,... | collective-permute-start | bytes 24584 | tf_op jit(solution)/shard_map/ppermute | solution.py:392
  255.8 3.7 collective-permute-start.26
  258.4 7.4 %copy-start.51 = (f32[4,1,256]{2,1,0:T(1,128)S(1)}, f32[4,1,256]{2,1,0:T(1,128)}, u32[]{:S(2)}) copy-start(f32[4,1,256]{2,1,0:T(1,128)} %get-tuple-element.46) | copy-start | bytes 12292
  258.4 7.4 %copy-start.49 = (f32[4,512]{1,0:T(4,128)S(1)}, f32[4,512]{1,0:T(4,128)}, u32[]{:S(2)}) copy-start(f32[4,512]{1,0:T(4,128)} %get-tuple-element.47) | copy-start | bytes 24580
  258.4 7.4 %copy-start.48 = (f32[4,512]{1,0:T(4,128)S(1)}, f32[4,512]{1,0:T(4,128)}, u32[]{:S(2)}) copy-start(f32[4,512]{1,0:T(4,128)} %get-tuple-element.48) | copy-start | bytes 24580
  258.4 7.5 %copy-start.46 = (f32[4,1024]{1,0:T(4,128)S(1)}, f32[4,1024]{1,0:T(4,128)}, u32[]{:S(2)}) copy-start(f32[4,1024]{1,0:T(4,128)} %get-tuple-element.49) | copy-start | bytes 49156
  259.5 3.7 collective-permute-start.27
  263.2 7.2 %collective-permute-start.28 = (bf16[64,8]{0,1:T(8,128)(2,1)S(1)}, bf16[64,8]{0,1:T(8,128)(2,1)S(1)}, u32[]{:S(2)}, u32[]{:S(2)}) collective-permute-start(bf16[64,8]{0,1:T(8,128)(2,1)S(1)} %fusion.51), channel_id=1, source_target_pairs={{0,16},{2,18},{4,20},{6,22},{8,24},{10,26},{12,28},{14,30},{16,0},... | collective-permute-start | bytes 3080 | tf_op jit(solution)/shard_map/ppermute | solution.py:392
  270.4 11.9 %collective-permute-start.9 = (bf16[2,2,2,64,512]{4,3,0,1,2:T(8,128)(2,1)S(1)}, bf16[2,2,2,64,512]{4,3,0,1,2:T(8,128)(2,1)S(1)}, u32[]{:S(2)}, u32[]{:S(2)}) collective-permute-start(bf16[2,2,2,64,512]{4,3,0,1,2:T(8,128)(2,1)S(1)} %bitcast.321), channel_id=1, source_target_pairs={{0,2},{2,0},{4,6},{6,4},{8,10},{10,8},{12,14},{14,12},{16,18},{18,... | collective-permute-start | bytes 1572872 | tf_op jit(solution)/shard_map/ppermute | solution.py:392
  271.0 13.9 %collective-permute-start.13 = (bf16[2,2,2,64,512]{4,3,2,0,1:T(8,128)(2,1)S(1)}, bf16[2,2,2,64,512]{4,3,2,0,1:T(8,128)(2,1)S(1)}, u32[]{:S(2)}, u32[]{:S(2)}) collective-permute-start(bf16[2,2,2,64,512]{4,3,2,0,1:T(8,128)(2,1)S(1)} %bitcast.320), channel_id=1, source_target_pairs={{0,2},{2,0},{4,6},{6,4},{8,10},{10,8},{12,14},{14,12},{16,18},{18,... | collective-permute-start | bytes 1572872 | tf_op jit(solution)/shard_map/ppermute | solution.py:392
  273.4 76.0 %collective-permute-start.17 = (bf16[2,2,2,64,1024]{4,3,0,1,2:T(8,128)(2,1)}, bf16[2,2,2,64,1024]{4,3,0,1,2:T(8,128)(2,1)}, u32[]{:S(2)}, u32[]{:S(2)}) collective-permute-start(bf16[2,2,2,64,1024]{4,3,0,1,2:T(8,128)(2,1)} %bitcast.301), channel_id=1, source_target_pairs={{0,2},{2,0},{4,6},{6,4},{8,10},{10,8},{12,14},{14,12},{16,18},{18,... | collective-permute-start | bytes 3145736 | tf_op jit(solution)/shard_map/ppermute | solution.py:392
  275.7 77.0 %collective-permute-start.21 = (bf16[2,2,2,64,1024]{4,3,2,0,1:T(8,128)(2,1)}, bf16[2,2,2,64,1024]{4,3,2,0,1:T(8,128)(2,1)}, u32[]{:S(2)}, u32[]{:S(2)}) collective-permute-start(bf16[2,2,2,64,1024]{4,3,2,0,1:T(8,128)(2,1)} %bitcast.300), channel_id=1, source_target_pairs={{0,2},{2,0},{4,6},{6,4},{8,10},{10,8},{12,14},{14,12},{16,18},{18,... | collective-permute-start | bytes 3145736 | tf_op jit(solution)/shard_map/ppermute | solution.py:392
  280.7 74.4 %collective-permute-start.29 = (bf16[2,2,2,64,1024]{4,3,2,0,1:T(8,128)(2,1)}, bf16[2,2,2,64,1024]{4,3,2,0,1:T(8,128)(2,1)}, u32[]{:S(2)}, u32[]{:S(2)}) collective-permute-start(bf16[2,2,2,64,1024]{4,3,2,0,1:T(8,128)(2,1)} %bitcast.299), channel_id=1, source_target_pairs={{0,2},{2,0},{4,6},{6,4},{8,10},{10,8},{12,14},{14,12},{16,18},{18,... | collective-permute-start | bytes 3145736 | tf_op jit(solution)/shard_map/ppermute | solution.py:392
  282.4 76.6 %collective-permute-start.34 = (bf16[2,2,64,1408]{3,2,0,1:T(8,128)(2,1)}, bf16[2,2,64,1408]{3,2,0,1:T(8,128)(2,1)}, u32[]{:S(2)}, u32[]{:S(2)}) collective-permute-start(bf16[2,2,64,1408]{3,2,0,1:T(8,128)(2,1)} %dynamic-slice_bitcast_fusion.2), channel_id=1, source_target_pairs={{0,4},{2,6},{4,0},{6,2},{8,12},{10,14},{12,8},{14,10},{16,20},{18,... | collective-permute-start | bytes 2162696 | tf_op jit(solution)/shard_map/ppermute | solution.py:392
  284.9 3.7 collective-permute-start.4
  287.4 16.3 %copy-start.30 = (bf16[2,2,2,64,512]{4,3,0,1,2:T(8,128)(2,1)S(1)}, bf16[2,2,2,64,512]{4,3,0,1,2:T(8,128)(2,1)}, u32[]{:S(2)}) copy-start(bf16[2,2,2,64,512]{4,3,0,1,2:T(8,128)(2,1)} %fusion.15) | copy-start | bytes 1572868
  288.7 1.2 collective-permute-start.5
  290.0 16.6 %copy-start.31 = (bf16[2,2,2,64,512]{4,3,2,0,1:T(8,128)(2,1)S(1)}, bf16[2,2,2,64,512]{4,3,2,0,1:T(8,128)(2,1)}, u32[]{:S(2)}) copy-start(bf16[2,2,2,64,512]{4,3,2,0,1:T(8,128)(2,1)} %fusion.14) | copy-start | bytes 1572868
  290.0 12.0 %collective-permute-start.6 = (f32[10504]{0:T(1024)S(1)}, f32[10504]{0:T(1024)S(1)}, u32[]{:S(2)}, u32[]{:S(2)}) collective-permute-start(f32[10504]{0:T(1024)S(1)} %add.364), channel_id=1, source_target_pairs={{0,4},{2,6},{4,0},{6,2},{8,12},{10,14},{12,8},{14,10},{16,20},{18,... | collective-permute-start | bytes 126056 | tf_op jit(solution)/shard_map/ppermute | solution.py:392
  302.0 4.1 collective-permute-start.7
  306.1 5.0 %collective-permute-start.8 = (f32[10504]{0:T(1024)S(1)}, f32[10504]{0:T(1024)S(1)}, u32[]{:S(2)}, u32[]{:S(2)}) collective-permute-start(f32[10504]{0:T(1024)S(1)} %add.366), channel_id=1, source_target_pairs={{0,16},{2,18},{4,20},{6,22},{8,24},{10,26},{12,28},{14,30},{16,0},... | collective-permute-start | bytes 126056 | tf_op jit(solution)/shard_map/ppermute | solution.py:392
  306.6 44.3 %copy-start.24 = (bf16[2,2,2,1,64,1024]{5,4,3,2,1,0:T(8,128)(2,1)S(1)}, bf16[2,2,2,1,64,1024]{5,4,3,2,1,0:T(8,128)(2,1)}, u32[]{:S(2)}) copy-start(bf16[2,2,2,1,64,1024]{5,4,3,2,1,0:T(8,128)(2,1)} %get-tuple-element.71) | copy-start | bytes 3145732
  311.1 6.4 %collective-permute-start.10 = (bf16[2,2,64,512]{3,2,0,1:T(8,128)(2,1)S(1)}, bf16[2,2,64,512]{3,2,0,1:T(8,128)(2,1)S(1)}, u32[]{:S(2)}, u32[]{:S(2)}) collective-permute-start(bf16[2,2,64,512]{3,2,0,1:T(8,128)(2,1)S(1)} %dynamic-slice_bitcast_fusion.15), channel_id=1, source_target_pairs={{0,4},{2,6},{4,0},{6,2},{8,12},{10,14},{12,8},{14,10},{16,20},{18,... | collective-permute-start | bytes 786440 | tf_op jit(solution)/shard_map/ppermute | solution.py:392
  317.5 7.8 %collective-permute-start.14 = (bf16[2,2,64,512]{3,2,1,0:T(8,128)(2,1)S(1)}, bf16[2,2,64,512]{3,2,1,0:T(8,128)(2,1)S(1)}, u32[]{:S(2)}, u32[]{:S(2)}) collective-permute-start(bf16[2,2,64,512]{3,2,1,0:T(8,128)(2,1)S(1)} %dynamic-slice_bitcast_fusion.14), channel_id=1, source_target_pairs={{0,8},{2,10},{4,12},{6,14},{8,0},{10,2},{12,4},{14,6},{16,24},{18,... | collective-permute-start | bytes 786440 | tf_op jit(solution)/shard_map/ppermute | solution.py:392
  325.3 5.4 %collective-permute-start.11 = (bf16[2,64,512]{2,1,0:T(8,128)(2,1)S(1)}, bf16[2,64,512]{2,1,0:T(8,128)(2,1)S(1)}, u32[]{:S(2)}, u32[]{:S(2)}) collective-permute-start(bf16[2,64,512]{2,1,0:T(8,128)(2,1)S(1)} %dynamic-slice_bitcast_fusion.23), channel_id=1, source_target_pairs={{0,8},{2,10},{4,12},{6,14},{8,0},{10,2},{12,4},{14,6},{16,24},{18,... | collective-permute-start | bytes 393224 | tf_op jit(solution)/shard_map/ppermute | solution.py:392
  330.7 7.7 %collective-permute-start.15 = (bf16[2,64,512]{2,1,0:T(8,128)(2,1)S(1)}, bf16[2,64,512]{2,1,0:T(8,128)(2,1)S(1)}, u32[]{:S(2)}, u32[]{:S(2)}) collective-permute-start(bf16[2,64,512]{2,1,0:T(8,128)(2,1)S(1)} %dynamic-slice_bitcast_fusion.22), channel_id=1, source_target_pairs={{0,16},{2,18},{4,20},{6,22},{8,24},{10,26},{12,28},{14,30},{16,0},... | collective-permute-start | bytes 393224 | tf_op jit(solution)/shard_map/ppermute | solution.py:392
  338.4 5.4 %collective-permute-start.12 = (bf16[64,512]{1,0:T(8,128)(2,1)S(1)}, bf16[64,512]{1,0:T(8,128)(2,1)S(1)}, u32[]{:S(2)}, u32[]{:S(2)}) collective-permute-start(bf16[64,512]{1,0:T(8,128)(2,1)S(1)} %dynamic-slice_bitcast_fusion.25), channel_id=1, source_target_pairs={{0,16},{2,18},{4,20},{6,22},{8,24},{10,26},{12,28},{14,30},{16,0},... | collective-permute-start | bytes 196616 | tf_op jit(solution)/shard_map/ppermute | solution.py:392
  343.8 5.0 %collective-permute-start.16 = (bf16[64,512]{1,0:T(8,128)(2,1)S(1)}, bf16[64,512]{1,0:T(8,128)(2,1)S(1)}, u32[]{:S(2)}, u32[]{:S(2)}) collective-permute-start(bf16[64,512]{1,0:T(8,128)(2,1)S(1)} %dynamic-slice_bitcast_fusion.24), channel_id=1, source_target_pairs={{0,4},{2,6},{4,0},{6,2},{8,12},{10,14},{12,8},{14,10},{16,20},{18,... | collective-permute-start | bytes 196616 | tf_op jit(solution)/shard_map/ppermute | solution.py:392
  348.7 23.1 %collective-permute-start.38 = (bf16[2,2,64,1408]{3,2,1,0:T(8,128)(2,1)}, bf16[2,2,64,1408]{3,2,1,0:T(8,128)(2,1)S(1)}, u32[]{:S(2)}, u32[]{:S(2)}) collective-permute-start(bf16[2,2,64,1408]{3,2,1,0:T(8,128)(2,1)} %dynamic-slice_bitcast_fusion.1), channel_id=1, source_target_pairs={{0,8},{2,10},{4,12},{6,14},{8,0},{10,2},{12,4},{14,6},{16,24},{18,... | collective-permute-start | bytes 2162696 | tf_op jit(solution)/shard_map/ppermute | solution.py:392
  349.4 22.7 %collective-permute-start.42 = (bf16[2,2,64,1408]{3,2,0,1:T(8,128)(2,1)}, bf16[2,2,64,1408]{3,2,0,1:T(8,128)(2,1)S(1)}, u32[]{:S(2)}, u32[]{:S(2)}) collective-permute-start(bf16[2,2,64,1408]{3,2,0,1:T(8,128)(2,1)} %dynamic-slice_bitcast_fusion), channel_id=1, source_target_pairs={{0,4},{2,6},{4,0},{6,2},{8,12},{10,14},{12,8},{14,10},{16,20},{18,... | collective-permute-start | bytes 2162696 | tf_op jit(solution)/shard_map/ppermute | solution.py:392
  352.7 62.3 %collective-permute-start.18 = (bf16[2,2,64,1024]{3,2,0,1:T(8,128)(2,1)S(1)}, bf16[2,2,64,1024]{3,2,0,1:T(8,128)(2,1)S(1)}, u32[]{:S(2)}, u32[]{:S(2)}) collective-permute-start(bf16[2,2,64,1024]{3,2,0,1:T(8,128)(2,1)S(1)} %dynamic-slice_bitcast_fusion.5), channel_id=1, source_target_pairs={{0,4},{2,6},{4,0},{6,2},{8,12},{10,14},{12,8},{14,10},{16,20},{18,... | collective-permute-start | bytes 1572872 | tf_op jit(solution)/shard_map/ppermute | solution.py:392
  355.1 61.0 %collective-permute-start.22 = (bf16[2,2,64,1024]{3,2,1,0:T(8,128)(2,1)S(1)}, bf16[2,2,64,1024]{3,2,1,0:T(8,128)(2,1)S(1)}, u32[]{:S(2)}, u32[]{:S(2)}) collective-permute-start(bf16[2,2,64,1024]{3,2,1,0:T(8,128)(2,1)S(1)} %dynamic-slice_bitcast_fusion.4), channel_id=1, source_target_pairs={{0,8},{2,10},{4,12},{6,14},{8,0},{10,2},{12,4},{14,6},{16,24},{18,... | collective-permute-start | bytes 1572872 | tf_op jit(solution)/shard_map/ppermute | solution.py:392
  358.9 12.9 %copy-start.14 = (bf16[2,2,2,64,1408]{4,3,2,0,1:T(8,128)(2,1)S(1)}, bf16[2,2,2,64,1408]{4,3,2,0,1:T(8,128)(2,1)}, u32[]{:S(2)}) copy-start(bf16[2,2,2,64,1408]{4,3,2,0,1:T(8,128)(2,1)} %copy-done.13) | copy-start | bytes 4325380
  359.0 59.9 %collective-permute-start.30 = (bf16[2,2,64,1024]{3,2,1,0:T(8,128)(2,1)S(1)}, bf16[2,2,64,1024]{3,2,1,0:T(8,128)(2,1)S(1)}, u32[]{:S(2)}, u32[]{:S(2)}) collective-permute-start(bf16[2,2,64,1024]{3,2,1,0:T(8,128)(2,1)S(1)} %dynamic-slice_bitcast_fusion.3), channel_id=1, source_target_pairs={{0,8},{2,10},{4,12},{6,14},{8,0},{10,2},{12,4},{14,6},{16,24},{18,... | collective-permute-start | bytes 1572872 | tf_op jit(solution)/shard_map/ppermute | solution.py:392
  360.4 14.1 %copy-start.16 = (bf16[2,2,2,64,1408]{4,3,0,1,2:T(8,128)(2,1)S(1)}, bf16[2,2,2,64,1408]{4,3,0,1,2:T(8,128)(2,1)}, u32[]{:S(2)}) copy-start(bf16[2,2,2,64,1408]{4,3,0,1,2:T(8,128)(2,1)} %copy-done.15) | copy-start | bytes 4325380
  371.8 28.3 %collective-permute-start.35 = (bf16[2,64,1408]{2,1,0:T(8,128)(2,1)S(1)}, bf16[2,64,1408]{2,1,0:T(8,128)(2,1)S(1)}, u32[]{:S(2)}, u32[]{:S(2)}) collective-permute-start(bf16[2,64,1408]{2,1,0:T(8,128)(2,1)S(1)} %dynamic-slice_bitcast_fusion.10), channel_id=1, source_target_pairs={{0,8},{2,10},{4,12},{6,14},{8,0},{10,2},{12,4},{14,6},{16,24},{18,... | collective-permute-start | bytes 1081352 | tf_op jit(solution)/shard_map/ppermute | solution.py:392
  372.1 29.3 %collective-permute-start.39 = (bf16[2,64,1408]{2,1,0:T(8,128)(2,1)S(1)}, bf16[2,64,1408]{2,1,0:T(8,128)(2,1)S(1)}, u32[]{:S(2)}, u32[]{:S(2)}) collective-permute-start(bf16[2,64,1408]{2,1,0:T(8,128)(2,1)S(1)} %dynamic-slice_bitcast_fusion.9), channel_id=1, source_target_pairs={{0,16},{2,18},{4,20},{6,22},{8,24},{10,26},{12,28},{14,30},{16,0},... | collective-permute-start | bytes 1081352 | tf_op jit(solution)/shard_map/ppermute | solution.py:392
  400.1 13.7 %collective-permute-start.43 = (bf16[2,64,1408]{2,1,0:T(8,128)(2,1)S(1)}, bf16[2,64,1408]{2,1,0:T(8,128)(2,1)S(1)}, u32[]{:S(2)}, u32[]{:S(2)}) collective-permute-start(bf16[2,64,1408]{2,1,0:T(8,128)(2,1)S(1)} %dynamic-slice_bitcast_fusion.8), channel_id=1, source_target_pairs={{0,8},{2,10},{4,12},{6,14},{8,0},{10,2},{12,4},{14,6},{16,24},{18,... | collective-permute-start | bytes 1081352 | tf_op jit(solution)/shard_map/ppermute | solution.py:392
  401.4 17.8 %collective-permute-start.36 = (bf16[64,1408]{1,0:T(8,128)(2,1)S(1)}, bf16[64,1408]{1,0:T(8,128)(2,1)S(1)}, u32[]{:S(2)}, u32[]{:S(2)}) collective-permute-start(bf16[64,1408]{1,0:T(8,128)(2,1)S(1)} %dynamic-slice_bitcast_fusion.18), channel_id=1, source_target_pairs={{0,16},{2,18},{4,20},{6,22},{8,24},{10,26},{12,28},{14,30},{16,0},... | collective-permute-start | bytes 540680 | tf_op jit(solution)/shard_map/ppermute | solution.py:392
  413.8 9.1 %collective-permute-start.40 = (bf16[64,1408]{1,0:T(8,128)(2,1)S(1)}, bf16[64,1408]{1,0:T(8,128)(2,1)S(1)}, u32[]{:S(2)}, u32[]{:S(2)}) collective-permute-start(bf16[64,1408]{1,0:T(8,128)(2,1)S(1)} %dynamic-slice_bitcast_fusion.17), channel_id=1, source_target_pairs={{0,4},{2,6},{4,0},{6,2},{8,12},{10,14},{12,8},{14,10},{16,20},{18,... | collective-permute-start | bytes 540680 | tf_op jit(solution)/shard_map/ppermute | solution.py:392
  415.0 15.8 %collective-permute-start.44 = (bf16[64,1408]{1,0:T(8,128)(2,1)S(1)}, bf16[64,1408]{1,0:T(8,128)(2,1)S(1)}, u32[]{:S(2)}, u32[]{:S(2)}) collective-permute-start(bf16[64,1408]{1,0:T(8,128)(2,1)S(1)} %dynamic-slice_bitcast_fusion.16), channel_id=1, source_target_pairs={{0,16},{2,18},{4,20},{6,22},{8,24},{10,26},{12,28},{14,30},{16,0},... | collective-permute-start | bytes 540680 | tf_op jit(solution)/shard_map/ppermute | solution.py:392
  416.1 15.5 %collective-permute-start.19 = (bf16[2,64,1024]{2,1,0:T(8,128)(2,1)S(1)}, bf16[2,64,1024]{2,1,0:T(8,128)(2,1)S(1)}, u32[]{:S(2)}, u32[]{:S(2)}) collective-permute-start(bf16[2,64,1024]{2,1,0:T(8,128)(2,1)S(1)} %dynamic-slice_bitcast_fusion.13), channel_id=1, source_target_pairs={{0,8},{2,10},{4,12},{6,14},{8,0},{10,2},{12,4},{14,6},{16,24},{18,... | collective-permute-start | bytes 786440 | tf_op jit(solution)/shard_map/ppermute | solution.py:392
  418.9 15.8 %collective-permute-start.23 = (bf16[2,64,1024]{2,1,0:T(8,128)(2,1)S(1)}, bf16[2,64,1024]{2,1,0:T(8,128)(2,1)S(1)}, u32[]{:S(2)}, u32[]{:S(2)}) collective-permute-start(bf16[2,64,1024]{2,1,0:T(8,128)(2,1)S(1)} %dynamic-slice_bitcast_fusion.12), channel_id=1, source_target_pairs={{0,16},{2,18},{4,20},{6,22},{8,24},{10,26},{12,28},{14,30},{16,0},... | collective-permute-start | bytes 786440 | tf_op jit(solution)/shard_map/ppermute | solution.py:392
  419.2 19.6 %collective-permute-start.31 = (bf16[2,64,1024]{2,1,0:T(8,128)(2,1)S(1)}, bf16[2,64,1024]{2,1,0:T(8,128)(2,1)S(1)}, u32[]{:S(2)}, u32[]{:S(2)}) collective-permute-start(bf16[2,64,1024]{2,1,0:T(8,128)(2,1)S(1)} %dynamic-slice_bitcast_fusion.11), channel_id=1, source_target_pairs={{0,16},{2,18},{4,20},{6,22},{8,24},{10,26},{12,28},{14,30},{16,0},... | collective-permute-start | bytes 786440 | tf_op jit(solution)/shard_map/ppermute | solution.py:392
  431.6 13.1 %copy-start.1 = (bf16[1024,1408]{1,0:T(8,128)(2,1)S(1)}, bf16[1024,1408]{1,0:T(8,128)(2,1)}, u32[]{:S(2)}) copy-start(bf16[1024,1408]{1,0:T(8,128)(2,1)} %param.38) | copy-start | bytes 8650756
  431.7 8.8 %collective-permute-start.20 = (bf16[64,1024]{1,0:T(8,128)(2,1)S(1)}, bf16[64,1024]{1,0:T(8,128)(2,1)S(1)}, u32[]{:S(2)}, u32[]{:S(2)}) collective-permute-start(bf16[64,1024]{1,0:T(8,128)(2,1)S(1)} %dynamic-slice_bitcast_fusion.21), channel_id=1, source_target_pairs={{0,16},{2,18},{4,20},{6,22},{8,24},{10,26},{12,28},{14,30},{16,0},... | collective-permute-start | bytes 393224 | tf_op jit(solution)/shard_map/ppermute | solution.py:392
  434.7 6.5 %collective-permute-start.24 = (bf16[64,1024]{1,0:T(8,128)(2,1)S(1)}, bf16[64,1024]{1,0:T(8,128)(2,1)S(1)}, u32[]{:S(2)}, u32[]{:S(2)}) collective-permute-start(bf16[64,1024]{1,0:T(8,128)(2,1)S(1)} %dynamic-slice_bitcast_fusion.20), channel_id=1, source_target_pairs={{0,4},{2,6},{4,0},{6,2},{8,12},{10,14},{12,8},{14,10},{16,20},{18,... | collective-permute-start | bytes 393224 | tf_op jit(solution)/shard_map/ppermute | solution.py:392
  438.9 5.0 %collective-permute-start.32 = (bf16[64,1024]{1,0:T(8,128)(2,1)S(1)}, bf16[64,1024]{1,0:T(8,128)(2,1)S(1)}, u32[]{:S(2)}, u32[]{:S(2)}) collective-permute-start(bf16[64,1024]{1,0:T(8,128)(2,1)S(1)} %dynamic-slice_bitcast_fusion.19), channel_id=1, source_target_pairs={{0,4},{2,6},{4,0},{6,2},{8,12},{10,14},{12,8},{14,10},{16,20},{18,... | collective-permute-start | bytes 393224 | tf_op jit(solution)/shard_map/ppermute | solution.py:392
  (49 other events, 150.6 us)
Sparse Core Ops, SparseCore 0:
  77.6 32.8 all-gather.1
